TPU v7x, 32 devices: a whole 2x2x4 slice. The times are simulated.
32 devices in a mesh: groups: 2 (over x), blk: 16 (over z, y, core).
Axes of the slice: x: 2, y: 2, z: 4, core: 2. Of those that a mesh axis runs over, the one named last changes fastest.
Arguments:
- rows: bfloat16 [131072, 768], P(('groups', 'blk')), parts along dimension 0, may hold values from -8 to 8, as said below
- centroids: bfloat16 [8192, 768], P(('groups', 'blk')), parts along dimension 0, may hold values from -4 to 4, as said below
- lists: int32 [512, 6], P(('groups', 'blk')), parts along dimension 0, may hold values from 0 to 15, as said below
Outputs:
- new_centroids: float32 [8192, 768], P(('groups', 'blk')), parts along dimension 0
- log_totals: float32 [131072], P(('groups', 'blk')), parts along dimension 0
There are 2 independent parts, one for each index of `groups`. A program takes and returns all parts, laid end to end along the dimension named above; each array names one. Nothing has to cross between parts.
Inputs may be any that keep to these rules, and one draw needn't show every extreme that they name: `rows`: embeddings of order one. `centroids`: centroids of order one half. `lists`: the 6 entries of a block are distinct panel numbers. Block b is held by device q = b // 16 along blk; every listed panel lies within cycle distance 6 of panel q (indices taken modulo 16), panel q itself is always listed, and distance 6 is reached. Panels are listed unevenly.
All inputs are finite; a program needn't handle non-finite values.
Results may differ from a plain program's by a relative error of at most 0.00056.
Values may be sent and summed in bfloat16 or wider, within the bound.
No kernel may reach another device: no remote copies, remote signals or barrier semaphores. Data moves between devices by JAX's collectives and lax.ppermute only.
A program may use at most 128 MiB of HBM per device.

v0:
```python
import jax
import jax.numpy as jnp
from jax import lax
from jax.sharding import PartitionSpec as P

BLOCK = 256
LISTED = 6
SPAN = 6


logit_scale = 0.25
prior_mass = 8.0


def passed_along(value, axis, steps):
    count = lax.axis_size(axis)
    pairs = [(source, (source + steps) % count) for source in range(count)]
    return lax.ppermute(value, axis, pairs)


def first_panel(panel):
    return passed_along(panel, "blk", SPAN)


def next_panel(panel):
    return passed_along(panel, "blk", -1)


def carry_onward(sums_pair):
    return passed_along((sums_pair[0], sums_pair[1]), "blk", 1)


def carry_to_owner(sums_pair):
    return passed_along((sums_pair[0], sums_pair[1]), "blk", -SPAN)


def log_partition(flat_rows_view):
    highest = jnp.max(flat_rows_view, axis=-1, keepdims=True)
    return highest[..., 0] + jnp.log(jnp.sum(jnp.exp(flat_rows_view - highest), axis=-1))


def on_device(rows, centroids, lists):
    cycle_size = lax.axis_size("blk")
    device = lax.axis_index("blk")
    cent_rows, width_dim = centroids.shape
    window_size = 2 * SPAN + 1
    moving = first_panel(centroids)
    pieces = [moving]
    for step_number in range(2 * SPAN):
        moving = next_panel(moving)
        pieces.append(moving)
    window = jnp.stack(pieces)
    norms = jnp.sum(jnp.square(window.astype(jnp.float32)), axis=-1)
    slot_ids = (lists - device + SPAN) % cycle_size
    block_count = rows.shape[0] // BLOCK
    grouped_rows = rows.reshape(block_count // 4, 4, BLOCK, width_dim)
    slot_groups = slot_ids.reshape(block_count // 4, 4, LISTED)
    slot_range = jnp.arange(window_size, dtype=jnp.int32)

    def score_group(running_counts, inputs):
        weighted_sums, weight_totals = running_counts
        block_rows, group_slots = inputs
        panels = window[group_slots]
        scores = jnp.einsum(
            "gbd,glcd->gblc", block_rows, panels, preferred_element_type=jnp.float32
        )
        logits = (scores - 0.5 * norms[group_slots][:, None]) * logit_scale
        flat_rows_view = logits.reshape(4, BLOCK, LISTED * cent_rows)
        log_total = log_partition(flat_rows_view)
        weights = jnp.exp(flat_rows_view - log_total[..., None]).astype(jnp.bfloat16)
        partial_value = jnp.einsum(
            "gbk,gbd->gkd", weights, block_rows, preferred_element_type=jnp.float32
        )
        partial_value = partial_value.reshape(4, LISTED, cent_rows, width_dim)
        summed_weights = jnp.sum(weights.astype(jnp.float32), axis=1).reshape(4, LISTED, cent_rows)
        slot_lookup_table = (group_slots[..., None] == slot_range).astype(jnp.float32)
        weighted_sums = weighted_sums + jnp.einsum(
            "glw,glcd->wcd", slot_lookup_table, partial_value, precision=lax.Precision.HIGHEST
        )
        weight_totals = weight_totals + jnp.einsum(
            "zhx,zhq->xq", slot_lookup_table, summed_weights, precision=lax.Precision.HIGHEST
        )
        return ((weighted_sums, weight_totals), log_total)

    start = (
        jnp.zeros((window_size, cent_rows, width_dim), jnp.float32),
        jnp.zeros((window_size, cent_rows), jnp.float32),
    )
    (weighted_sums, weight_totals), log_totals = lax.scan(
        score_group, start, (grouped_rows, slot_groups)
    )
    carried_sums = weighted_sums[2 * SPAN]
    carried_totals = weight_totals[2 * SPAN]
    for step_number in range(2 * SPAN):
        carried_sums, carried_totals = carry_onward((carried_sums, carried_totals))
        slot = 2 * SPAN - 1 - step_number
        carried_sums = carried_sums + weighted_sums[slot]
        carried_totals = carried_totals + weight_totals[slot]
    own_sums, own_totals = carry_to_owner((carried_sums, carried_totals))
    updated = (own_sums + prior_mass * centroids.astype(jnp.float32)) / (
        own_totals[:, None] + prior_mass
    )
    return (updated, log_totals.reshape(rows.shape[0]))


def solution(mesh):
    placed = (P(("groups", "blk"), None), P(("groups", "blk"), None), P(("groups", "blk"), None))
    return jax.shard_map(
        on_device,
        mesh=mesh,
        in_specs=placed,
        out_specs=(P(("groups", "blk"), None), P(("groups", "blk"))),
        check_vma=False,
    )
```

profile of v0, /device:TPU:0, one launch (start us, length us, event | category | flops | bytes accessed | tf_op | source)
XLA Modules:
  0.0 621.1 jit_solution(9672659691382637692)
XLA Ops:
  4.7 18.8 %collective-permute-done = bf16[256,768]{1,0:T(8,128)(2,1)S(1)} collective-permute-done((bf16[256,768]{1,0:T(8,128)(2,1)}, bf16[256,768]{1,0:T(8,128)(2,1)S(1)}, u32[]{:S(2)}, u32[]{:S(2)}) %collective-permute-start) | collective-permute-done | bytes 393248 | tf_op jit(solution)/shard_map/ppermute | solution.py:18
  140.0 215.9 %while.15 = (s32[]{:T(128)}, f32[13,256,768]{2,0,1:T(8,128)}, f32[13,256]{1,0:T(8,128)S(1)}, f32[4,4,256]{2,1,0:T(4,128)S(1)}, s32[4,4,6]{2,1,0:T(4,128)S(1)}, /...) while((s32[]{:T(128)}, f32[13,256,768]{2,0,1:T(8,128)}, ...), condition=%wide.region_5.6_spmd.clone, body=%wide.region_1.5_spmd.clone.sunk | while | flops 5591318016 | bytes 121400488 | solution.py:89
  140.7 8.3 %gather_fusion.1 = bf16[24,256,768]{2,1,0:T(8,128)(2,1)} fusion(bf16[13,256,768]{2,1,0:T(8,128)(2,1)} %get-tuple-element.199, s32[1024]{0:T(1024)S(1)} %pad_clamp_fusion.2), kind=kCustom, calls=%fused_computation.clone.clone.1 | custom fusion | bytes 18874464 | tf_op jit(solution)/shard_map/while/body/eval_jaxpr/gather | solution.py:63
  149.0 5.7 fusion.54
  162.0 30.6 %bitcast_add_fusion.2 = f32[13,256,768]{2,0,1:T(8,128)} fusion(f32[13,256,768]{2,0,1:T(8,128)} %get-tuple-element.184, pred[]{:T(512)S(6)} %compare.4, f32[4,6,256,768]{3,2,1,0:T(8,128)S(1)} %bitcast.160, s32[4,6]{1,0:T(4,128)S(1)} %dynamic-slice_bitcast_fusion.2), kind=kOutput, calls=%fused_computation.5.clone.1 | convolution fusion | flops 741212480 | bytes 39321696 | tf_op jit(solution)/shard_map/while/body/eval_jaxpr/glw,glcd->wcd/dot_general | solution.py:77
  193.3 8.3 %gather_fusion.1 = bf16[24,256,768]{2,1,0:T(8,128)(2,1)} fusion(bf16[13,256,768]{2,1,0:T(8,128)(2,1)} %get-tuple-element.199, s32[1024]{0:T(1024)S(1)} %pad_clamp_fusion.2), kind=kCustom, calls=%fused_computation.clone.clone.1 | custom fusion | bytes 18874464 | tf_op jit(solution)/shard_map/while/body/eval_jaxpr/gather | solution.py:63
  201.6 5.7 fusion.54
  214.6 32.4 %bitcast_add_fusion.2 = f32[13,256,768]{2,0,1:T(8,128)} fusion(f32[13,256,768]{2,0,1:T(8,128)} %get-tuple-element.184, pred[]{:T(512)S(6)} %compare.4, f32[4,6,256,768]{3,2,1,0:T(8,128)S(1)} %bitcast.160, s32[4,6]{1,0:T(4,128)S(1)} %dynamic-slice_bitcast_fusion.2), kind=kOutput, calls=%fused_computation.5.clone.1 | convolution fusion | flops 741212480 | bytes 39321696 | tf_op jit(solution)/shard_map/while/body/eval_jaxpr/glw,glcd->wcd/dot_general | solution.py:77
  247.8 8.3 %gather_fusion.1 = bf16[24,256,768]{2,1,0:T(8,128)(2,1)} fusion(bf16[13,256,768]{2,1,0:T(8,128)(2,1)} %get-tuple-element.199, s32[1024]{0:T(1024)S(1)} %pad_clamp_fusion.2), kind=kCustom, calls=%fused_computation.clone.clone.1 | custom fusion | bytes 18874464 | tf_op jit(solution)/shard_map/while/body/eval_jaxpr/gather | solution.py:63
  256.0 5.7 fusion.54
  269.1 32.4 %bitcast_add_fusion.2 = f32[13,256,768]{2,0,1:T(8,128)} fusion(f32[13,256,768]{2,0,1:T(8,128)} %get-tuple-element.184, pred[]{:T(512)S(6)} %compare.4, f32[4,6,256,768]{3,2,1,0:T(8,128)S(1)} %bitcast.160, s32[4,6]{1,0:T(4,128)S(1)} %dynamic-slice_bitcast_fusion.2), kind=kOutput, calls=%fused_computation.5.clone.1 | convolution fusion | flops 741212480 | bytes 39321696 | tf_op jit(solution)/shard_map/while/body/eval_jaxpr/glw,glcd->wcd/dot_general | solution.py:77
  302.2 8.3 %gather_fusion.1 = bf16[24,256,768]{2,1,0:T(8,128)(2,1)} fusion(bf16[13,256,768]{2,1,0:T(8,128)(2,1)} %get-tuple-element.199, s32[1024]{0:T(1024)S(1)} %pad_clamp_fusion.2), kind=kCustom, calls=%fused_computation.clone.clone.1 | custom fusion | bytes 18874464 | tf_op jit(solution)/shard_map/while/body/eval_jaxpr/gather | solution.py:63
  310.5 5.7 fusion.54
  323.5 32.4 %bitcast_add_fusion.2 = f32[13,256,768]{2,0,1:T(8,128)} fusion(f32[13,256,768]{2,0,1:T(8,128)} %get-tuple-element.184, pred[]{:T(512)S(6)} %compare.4, f32[4,6,256,768]{3,2,1,0:T(8,128)S(1)} %bitcast.160, s32[4,6]{1,0:T(4,128)S(1)} %dynamic-slice_bitcast_fusion.2), kind=kOutput, calls=%fused_computation.5.clone.1 | convolution fusion | flops 741212480 | bytes 39321696 | tf_op jit(solution)/shard_map/while/body/eval_jaxpr/glw,glcd->wcd/dot_general | solution.py:77
  355.9 10.5 %copy.22 = f32[13,256,768]{2,1,0:T(8,128)S(1)} copy(f32[13,256,768]{2,0,1:T(8,128)} %get-tuple-element.51) | data formatting | bytes 20447232 | tf_op jit(solution)/shard_map/while | solution.py:89
  366.5 14.2 %collective-permute-done.13 = f32[256,768]{1,0:T(8,128)S(1)} collective-permute-done((f32[256,768]{1,0:T(8,128)S(1)}, f32[256,768]{1,0:T(8,128)S(1)}, u32[]{:S(2)}, u32[]{:S(2)}) %collective-permute-start.13) | collective-permute-done | bytes 786464 | tf_op jit(solution)/shard_map/ppermute | solution.py:18
  380.9 14.1 %collective-permute-done.14 = f32[256,768]{1,0:T(8,128)S(1)} collective-permute-done((f32[256,768]{1,0:T(8,128)S(1)}, f32[256,768]{1,0:T(8,128)S(1)}, u32[]{:S(2)}, u32[]{:S(2)}) %collective-permute-start.14) | collective-permute-done | bytes 786464 | tf_op jit(solution)/shard_map/ppermute | solution.py:18
  395.2 14.1 %collective-permute-done.15 = f32[256,768]{1,0:T(8,128)S(1)} collective-permute-done((f32[256,768]{1,0:T(8,128)S(1)}, f32[256,768]{1,0:T(8,128)S(1)}, u32[]{:S(2)}, u32[]{:S(2)}) %collective-permute-start.15) | collective-permute-done | bytes 786464 | tf_op jit(solution)/shard_map/ppermute | solution.py:18
  409.4 14.1 %collective-permute-done.16 = f32[256,768]{1,0:T(8,128)S(1)} collective-permute-done((f32[256,768]{1,0:T(8,128)S(1)}, f32[256,768]{1,0:T(8,128)S(1)}, u32[]{:S(2)}, u32[]{:S(2)}) %collective-permute-start.16) | collective-permute-done | bytes 786464 | tf_op jit(solution)/shard_map/ppermute | solution.py:18
  423.7 14.1 %collective-permute-done.17 = f32[256,768]{1,0:T(8,128)S(1)} collective-permute-done((f32[256,768]{1,0:T(8,128)S(1)}, f32[256,768]{1,0:T(8,128)S(1)}, u32[]{:S(2)}, u32[]{:S(2)}) %collective-permute-start.17) | collective-permute-done | bytes 786464 | tf_op jit(solution)/shard_map/ppermute | solution.py:18
  438.0 14.1 %collective-permute-done.18 = f32[256,768]{1,0:T(8,128)S(1)} collective-permute-done((f32[256,768]{1,0:T(8,128)S(1)}, f32[256,768]{1,0:T(8,128)S(1)}, u32[]{:S(2)}, u32[]{:S(2)}) %collective-permute-start.18) | collective-permute-done | bytes 786464 | tf_op jit(solution)/shard_map/ppermute | solution.py:18
  452.3 14.1 %collective-permute-done.19 = f32[256,768]{1,0:T(8,128)S(1)} collective-permute-done((f32[256,768]{1,0:T(8,128)S(1)}, f32[256,768]{1,0:T(8,128)S(1)}, u32[]{:S(2)}, u32[]{:S(2)}) %collective-permute-start.19) | collective-permute-done | bytes 786464 | tf_op jit(solution)/shard_map/ppermute | solution.py:18
  466.5 14.1 %collective-permute-done.20 = f32[256,768]{1,0:T(8,128)S(1)} collective-permute-done((f32[256,768]{1,0:T(8,128)S(1)}, f32[256,768]{1,0:T(8,128)S(1)}, u32[]{:S(2)}, u32[]{:S(2)}) %collective-permute-start.20) | collective-permute-done | bytes 786464 | tf_op jit(solution)/shard_map/ppermute | solution.py:18
  480.8 14.1 %collective-permute-done.21 = f32[256,768]{1,0:T(8,128)S(1)} collective-permute-done((f32[256,768]{1,0:T(8,128)S(1)}, f32[256,768]{1,0:T(8,128)S(1)}, u32[]{:S(2)}, u32[]{:S(2)}) %collective-permute-start.21) | collective-permute-done | bytes 786464 | tf_op jit(solution)/shard_map/ppermute | solution.py:18
  495.1 14.2 %collective-permute-done.22 = f32[256,768]{1,0:T(8,128)S(1)} collective-permute-done((f32[256,768]{1,0:T(8,128)S(1)}, f32[256,768]{1,0:T(8,128)S(1)}, u32[]{:S(2)}, u32[]{:S(2)}) %collective-permute-start.22) | collective-permute-done | bytes 786464 | tf_op jit(solution)/shard_map/ppermute | solution.py:18
  509.5 14.2 %collective-permute-done.23 = f32[256,768]{1,0:T(8,128)S(1)} collective-permute-done((f32[256,768]{1,0:T(8,128)S(1)}, f32[256,768]{1,0:T(8,128)S(1)}, u32[]{:S(2)}, u32[]{:S(2)}) %collective-permute-start.23) | collective-permute-done | bytes 786464 | tf_op jit(solution)/shard_map/ppermute | solution.py:18
  523.8 20.1 %collective-permute-done.24 = f32[256,768]{1,0:T(8,128)S(1)} collective-permute-done((f32[256,768]{1,0:T(8,128)S(1)}, f32[256,768]{1,0:T(8,128)S(1)}, u32[]{:S(2)}, u32[]{:S(2)}) %collective-permute-start.24) | collective-permute-done | bytes 786464 | tf_op jit(solution)/shard_map/ppermute | solution.py:18
  544.2 8.8 %collective-permute-done.26 = f32[256]{0:T(256)S(1)} collective-permute-done((f32[256]{0:T(256)S(1)}, f32[256]{0:T(256)S(1)}, u32[]{:S(2)}, u32[]{:S(2)}) %collective-permute-start.26) | collective-permute-done | bytes 1056 | tf_op jit(solution)/shard_map/ppermute | solution.py:18
  553.0 5.7 collective-permute-done.27
  570.1 5.7 collective-permute-done.30
  575.8 5.7 collective-permute-done.31
  581.5 5.7 collective-permute-done.32
  (164 shorter events, 200.1 us)
Async XLA Ops:
  0.6 22.8 %collective-permute-start = (bf16[256,768]{1,0:T(8,128)(2,1)}, bf16[256,768]{1,0:T(8,128)(2,1)S(1)}, u32[]{:S(2)}, u32[]{:S(2)}) collective-permute-start(bf16[256,768]{1,0:T(8,128)(2,1)} %param.6), channel_id=1, source_target_pairs={{0,6},{1,7},{2,8},{3,9},{4,10},{5,11},{6,12},{7,13},{8,14},{9,15},... | collective-permute-start | bytes 1179656 | tf_op jit(solution)/shard_map/ppermute | solution.py:18
  28.7 9.9 %collective-permute-start.2 = (bf16[256,768]{1,0:T(8,128)(2,1)S(1)}, bf16[256,768]{1,0:T(8,128)(2,1)S(1)}, u32[]{:S(2)}, u32[]{:S(2)}) collective-permute-start(bf16[256,768]{1,0:T(8,128)(2,1)S(1)} %collective-permute-done.1), channel_id=1, source_target_pairs={{0,15},{1,0},{2,1},{3,2},{4,3},{5,4},{6,5},{7,6},{8,7},{9,8},{10,9... | collective-permute-start | bytes 1179656 | tf_op jit(solution)/shard_map/ppermute | solution.py:18
  38.6 9.9 %collective-permute-start.3 = (bf16[256,768]{1,0:T(8,128)(2,1)S(1)}, bf16[256,768]{1,0:T(8,128)(2,1)S(1)}, u32[]{:S(2)}, u32[]{:S(2)}) collective-permute-start(bf16[256,768]{1,0:T(8,128)(2,1)S(1)} %collective-permute-done.2), channel_id=1, source_target_pairs={{0,15},{1,0},{2,1},{3,2},{4,3},{5,4},{6,5},{7,6},{8,7},{9,8},{10,9... | collective-permute-start | bytes 1179656 | tf_op jit(solution)/shard_map/ppermute | solution.py:18
  48.5 9.9 %collective-permute-start.4 = (bf16[256,768]{1,0:T(8,128)(2,1)S(1)}, bf16[256,768]{1,0:T(8,128)(2,1)S(1)}, u32[]{:S(2)}, u32[]{:S(2)}) collective-permute-start(bf16[256,768]{1,0:T(8,128)(2,1)S(1)} %collective-permute-done.3), channel_id=1, source_target_pairs={{0,15},{1,0},{2,1},{3,2},{4,3},{5,4},{6,5},{7,6},{8,7},{9,8},{10,9... | collective-permute-start | bytes 1179656 | tf_op jit(solution)/shard_map/ppermute | solution.py:18
  58.4 9.9 %collective-permute-start.5 = (bf16[256,768]{1,0:T(8,128)(2,1)S(1)}, bf16[256,768]{1,0:T(8,128)(2,1)S(1)}, u32[]{:S(2)}, u32[]{:S(2)}) collective-permute-start(bf16[256,768]{1,0:T(8,128)(2,1)S(1)} %collective-permute-done.4), channel_id=1, source_target_pairs={{0,15},{1,0},{2,1},{3,2},{4,3},{5,4},{6,5},{7,6},{8,7},{9,8},{10,9... | collective-permute-start | bytes 1179656 | tf_op jit(solution)/shard_map/ppermute | solution.py:18
  68.3 9.9 %collective-permute-start.6 = (bf16[256,768]{1,0:T(8,128)(2,1)S(1)}, bf16[256,768]{1,0:T(8,128)(2,1)S(1)}, u32[]{:S(2)}, u32[]{:S(2)}) collective-permute-start(bf16[256,768]{1,0:T(8,128)(2,1)S(1)} %collective-permute-done.5), channel_id=1, source_target_pairs={{0,15},{1,0},{2,1},{3,2},{4,3},{5,4},{6,5},{7,6},{8,7},{9,8},{10,9... | collective-permute-start | bytes 1179656 | tf_op jit(solution)/shard_map/ppermute | solution.py:18
  78.2 9.9 %collective-permute-start.7 = (bf16[256,768]{1,0:T(8,128)(2,1)S(1)}, bf16[256,768]{1,0:T(8,128)(2,1)S(1)}, u32[]{:S(2)}, u32[]{:S(2)}) collective-permute-start(bf16[256,768]{1,0:T(8,128)(2,1)S(1)} %collective-permute-done.6), channel_id=1, source_target_pairs={{0,15},{1,0},{2,1},{3,2},{4,3},{5,4},{6,5},{7,6},{8,7},{9,8},{10,9... | collective-permute-start | bytes 1179656 | tf_op jit(solution)/shard_map/ppermute | solution.py:18
  88.1 9.9 %collective-permute-start.8 = (bf16[256,768]{1,0:T(8,128)(2,1)S(1)}, bf16[256,768]{1,0:T(8,128)(2,1)S(1)}, u32[]{:S(2)}, u32[]{:S(2)}) collective-permute-start(bf16[256,768]{1,0:T(8,128)(2,1)S(1)} %collective-permute-done.7), channel_id=1, source_target_pairs={{0,15},{1,0},{2,1},{3,2},{4,3},{5,4},{6,5},{7,6},{8,7},{9,8},{10,9... | collective-permute-start | bytes 1179656 | tf_op jit(solution)/shard_map/ppermute | solution.py:18
  98.0 9.9 %collective-permute-start.9 = (bf16[256,768]{1,0:T(8,128)(2,1)S(1)}, bf16[256,768]{1,0:T(8,128)(2,1)S(1)}, u32[]{:S(2)}, u32[]{:S(2)}) collective-permute-start(bf16[256,768]{1,0:T(8,128)(2,1)S(1)} %collective-permute-done.8), channel_id=1, source_target_pairs={{0,15},{1,0},{2,1},{3,2},{4,3},{5,4},{6,5},{7,6},{8,7},{9,8},{10,9... | collective-permute-start | bytes 1179656 | tf_op jit(solution)/shard_map/ppermute | solution.py:18
  107.9 9.9 %collective-permute-start.10 = (bf16[256,768]{1,0:T(8,128)(2,1)S(1)}, bf16[256,768]{1,0:T(8,128)(2,1)S(1)}, u32[]{:S(2)}, u32[]{:S(2)}) collective-permute-start(bf16[256,768]{1,0:T(8,128)(2,1)S(1)} %collective-permute-done.9), channel_id=1, source_target_pairs={{0,15},{1,0},{2,1},{3,2},{4,3},{5,4},{6,5},{7,6},{8,7},{9,8},{10,9... | collective-permute-start | bytes 1179656 | tf_op jit(solution)/shard_map/ppermute | solution.py:18
  117.8 9.9 %collective-permute-start.11 = (bf16[256,768]{1,0:T(8,128)(2,1)S(1)}, bf16[256,768]{1,0:T(8,128)(2,1)S(1)}, u32[]{:S(2)}, u32[]{:S(2)}) collective-permute-start(bf16[256,768]{1,0:T(8,128)(2,1)S(1)} %collective-permute-done.10), channel_id=1, source_target_pairs={{0,15},{1,0},{2,1},{3,2},{4,3},{5,4},{6,5},{7,6},{8,7},{9,8},{10,9... | collective-permute-start | bytes 1179656 | tf_op jit(solution)/shard_map/ppermute | solution.py:18
  127.7 9.9 %collective-permute-start.12 = (bf16[256,768]{1,0:T(8,128)(2,1)S(1)}, bf16[256,768]{1,0:T(8,128)(2,1)S(1)}, u32[]{:S(2)}, u32[]{:S(2)}) collective-permute-start(bf16[256,768]{1,0:T(8,128)(2,1)S(1)} %collective-permute-done.11), channel_id=1, source_target_pairs={{0,15},{1,0},{2,1},{3,2},{4,3},{5,4},{6,5},{7,6},{8,7},{9,8},{10,9... | collective-permute-start | bytes 1179656 | tf_op jit(solution)/shard_map/ppermute | solution.py:18
  366.5 14.2 %collective-permute-start.13 = (f32[256,768]{1,0:T(8,128)S(1)}, f32[256,768]{1,0:T(8,128)S(1)}, u32[]{:S(2)}, u32[]{:S(2)}) collective-permute-start(f32[256,768]{1,0:T(8,128)S(1)} %slice_bitcast_fusion.12), channel_id=1, source_target_pairs={{0,1},{1,2},{2,3},{3,4},{4,5},{5,6},{6,7},{7,8},{8,9},{9,10},{10,1... | collective-permute-start | bytes 2359304 | tf_op jit(solution)/shard_map/ppermute | solution.py:18
  380.8 14.2 %collective-permute-start.14 = (f32[256,768]{1,0:T(8,128)S(1)}, f32[256,768]{1,0:T(8,128)S(1)}, u32[]{:S(2)}, u32[]{:S(2)}) collective-permute-start(f32[256,768]{1,0:T(8,128)S(1)} %fusion.31), channel_id=1, source_target_pairs={{0,1},{1,2},{2,3},{3,4},{4,5},{5,6},{6,7},{7,8},{8,9},{9,10},{10,1... | collective-permute-start | bytes 2359304 | tf_op jit(solution)/shard_map/ppermute | solution.py:18
  395.1 14.2 %collective-permute-start.15 = (f32[256,768]{1,0:T(8,128)S(1)}, f32[256,768]{1,0:T(8,128)S(1)}, u32[]{:S(2)}, u32[]{:S(2)}) collective-permute-start(f32[256,768]{1,0:T(8,128)S(1)} %fusion.30), channel_id=1, source_target_pairs={{0,1},{1,2},{2,3},{3,4},{4,5},{5,6},{6,7},{7,8},{8,9},{9,10},{10,1... | collective-permute-start | bytes 2359304 | tf_op jit(solution)/shard_map/ppermute | solution.py:18
  409.4 14.2 %collective-permute-start.16 = (f32[256,768]{1,0:T(8,128)S(1)}, f32[256,768]{1,0:T(8,128)S(1)}, u32[]{:S(2)}, u32[]{:S(2)}) collective-permute-start(f32[256,768]{1,0:T(8,128)S(1)} %fusion.29), channel_id=1, source_target_pairs={{0,1},{1,2},{2,3},{3,4},{4,5},{5,6},{6,7},{7,8},{8,9},{9,10},{10,1... | collective-permute-start | bytes 2359304 | tf_op jit(solution)/shard_map/ppermute | solution.py:18
  423.6 14.2 %collective-permute-start.17 = (f32[256,768]{1,0:T(8,128)S(1)}, f32[256,768]{1,0:T(8,128)S(1)}, u32[]{:S(2)}, u32[]{:S(2)}) collective-permute-start(f32[256,768]{1,0:T(8,128)S(1)} %fusion.28), channel_id=1, source_target_pairs={{0,1},{1,2},{2,3},{3,4},{4,5},{5,6},{6,7},{7,8},{8,9},{9,10},{10,1... | collective-permute-start | bytes 2359304 | tf_op jit(solution)/shard_map/ppermute | solution.py:18
  437.9 14.2 %collective-permute-start.18 = (f32[256,768]{1,0:T(8,128)S(1)}, f32[256,768]{1,0:T(8,128)S(1)}, u32[]{:S(2)}, u32[]{:S(2)}) collective-permute-start(f32[256,768]{1,0:T(8,128)S(1)} %fusion.27), channel_id=1, source_target_pairs={{0,1},{1,2},{2,3},{3,4},{4,5},{5,6},{6,7},{7,8},{8,9},{9,10},{10,1... | collective-permute-start | bytes 2359304 | tf_op jit(solution)/shard_map/ppermute | solution.py:18
  452.2 14.2 %collective-permute-start.19 = (f32[256,768]{1,0:T(8,128)S(1)}, f32[256,768]{1,0:T(8,128)S(1)}, u32[]{:S(2)}, u32[]{:S(2)}) collective-permute-start(f32[256,768]{1,0:T(8,128)S(1)} %fusion.26), channel_id=1, source_target_pairs={{0,1},{1,2},{2,3},{3,4},{4,5},{5,6},{6,7},{7,8},{8,9},{9,10},{10,1... | collective-permute-start | bytes 2359304 | tf_op jit(solution)/shard_map/ppermute | solution.py:18
  466.5 14.2 %collective-permute-start.20 = (f32[256,768]{1,0:T(8,128)S(1)}, f32[256,768]{1,0:T(8,128)S(1)}, u32[]{:S(2)}, u32[]{:S(2)}) collective-permute-start(f32[256,768]{1,0:T(8,128)S(1)} %fusion.25), channel_id=1, source_target_pairs={{0,1},{1,2},{2,3},{3,4},{4,5},{5,6},{6,7},{7,8},{8,9},{9,10},{10,1... | collective-permute-start | bytes 2359304 | tf_op jit(solution)/shard_map/ppermute | solution.py:18
  480.7 14.2 %collective-permute-start.21 = (f32[256,768]{1,0:T(8,128)S(1)}, f32[256,768]{1,0:T(8,128)S(1)}, u32[]{:S(2)}, u32[]{:S(2)}) collective-permute-start(f32[256,768]{1,0:T(8,128)S(1)} %fusion.24), channel_id=1, source_target_pairs={{0,1},{1,2},{2,3},{3,4},{4,5},{5,6},{6,7},{7,8},{8,9},{9,10},{10,1... | collective-permute-start | bytes 2359304 | tf_op jit(solution)/shard_map/ppermute | solution.py:18
  495.0 14.3 %collective-permute-start.22 = (f32[256,768]{1,0:T(8,128)S(1)}, f32[256,768]{1,0:T(8,128)S(1)}, u32[]{:S(2)}, u32[]{:S(2)}) collective-permute-start(f32[256,768]{1,0:T(8,128)S(1)} %fusion.23), channel_id=1, source_target_pairs={{0,1},{1,2},{2,3},{3,4},{4,5},{5,6},{6,7},{7,8},{8,9},{9,10},{10,1... | collective-permute-start | bytes 2359304 | tf_op jit(solution)/shard_map/ppermute | solution.py:18
  509.4 14.3 %collective-permute-start.23 = (f32[256,768]{1,0:T(8,128)S(1)}, f32[256,768]{1,0:T(8,128)S(1)}, u32[]{:S(2)}, u32[]{:S(2)}) collective-permute-start(f32[256,768]{1,0:T(8,128)S(1)} %fusion.22), channel_id=1, source_target_pairs={{0,1},{1,2},{2,3},{3,4},{4,5},{5,6},{6,7},{7,8},{8,9},{9,10},{10,1... | collective-permute-start | bytes 2359304 | tf_op jit(solution)/shard_map/ppermute | solution.py:18
  523.8 20.1 %collective-permute-start.24 = (f32[256,768]{1,0:T(8,128)S(1)}, f32[256,768]{1,0:T(8,128)S(1)}, u32[]{:S(2)}, u32[]{:S(2)}) collective-permute-start(f32[256,768]{1,0:T(8,128)S(1)} %fusion.21), channel_id=1, source_target_pairs={{0,1},{1,2},{2,3},{3,4},{4,5},{5,6},{6,7},{7,8},{8,9},{9,10},{10,1... | collective-permute-start | bytes 2359304 | tf_op jit(solution)/shard_map/ppermute | solution.py:18
  544.0 76.1 %collective-permute-start.25 = (f32[256,768]{1,0:T(8,128)S(1)}, f32[256,768]{1,0:T(8,128)S(1)}, u32[]{:S(2)}, u32[]{:S(2)}) collective-permute-start(f32[256,768]{1,0:T(8,128)S(1)} %fusion.20), channel_id=1, source_target_pairs={{0,10},{1,11},{2,12},{3,13},{4,14},{5,15},{6,0},{7,1},{8,2},{9,3},... | collective-permute-start | bytes 2359304 | tf_op jit(solution)/shard_map/ppermute | solution.py:18
  544.1 8.9 %collective-permute-start.26 = (f32[256]{0:T(256)S(1)}, f32[256]{0:T(256)S(1)}, u32[]{:S(2)}, u32[]{:S(2)}) collective-permute-start(f32[256]{0:T(256)S(1)} %bitcast.178), channel_id=1, source_target_pairs={{0,1},{1,2},{2,3},{3,4},{4,5},{5,6},{6,7},{7,8},{8,9},{9,10},{10,1... | collective-permute-start | bytes 3080 | tf_op jit(solution)/shard_map/ppermute | solution.py:18
  570.1 5.7 collective-permute-start.30
  575.8 5.7 collective-permute-start.31
  581.5 5.7 collective-permute-start.32
  587.2 5.7 collective-permute-start.33
  604.3 5.7 collective-permute-start.36
  610.0 5.7 collective-permute-start.37
  (9 other events, 194.2 us)
where the time goes:
time: 622 us; the launch traced here: 621 us
  waiting for transfers between devices  332 us (53%)
  matrix products  168 us (27%)
  starting transfers between devices  55.5 us (9%)
  local copies, waits for them, and re-layouts  49.3 us (8%)
  other arithmetic  15.5 us (2%)
    ppermute x39, waiting for transfers between devices, passed_along(): return lax.ppermute(value, axis, pairs)  332 us
    dot_general x4, matrix products, score_group(): jnp.einsum('glw,glcd->wcd', slot_lookup_table, partial_value, precision=l...  128 us
    ppermute x39, starting transfers between devices, passed_along(): return lax.ppermute(value, axis, pairs)  55.5 us
    gather x4, local copies, waits for them, and re-layouts, score_group(): panels = window[group_slots]  33 us
    dot_general x4, matrix products, score_group(): jnp.einsum('gbd,glcd->gblc', block_rows, panels, preferred_element_type=j...  22.8 us
    dot_general x4, matrix products, score_group(): jnp.einsum('gbk,gbd->gkd', weights, block_rows, preferred_element_type=jn...  16.1 us
  transfers between devices with their start and end apart: 39, of which 38 were waited for; matrix products, arithmetic and copies ran while one was open for 0% of the time, Pallas kernels for 0%

commit v1 on v0

v1 whole, which is shorter than its diff:
```python
import math

import jax
import jax.numpy as jnp
from jax import lax
from jax.experimental import pallas as pl
from jax.experimental.pallas import tpu as pltpu
from jax.sharding import PartitionSpec as P

BLOCK = 256
SPAN = 6
LOGIT_SCALE = 0.25
PRIOR_MASS = 8.0
LOG2E = math.log2(math.e)
LINK_SCALE = 1.0 / 16.0
CHUNKS = 2


def permuted(value, target):
    count = lax.axis_size("blk")
    return lax.ppermute(value, "blk", [(i, target(i, count)) for i in range(count)])


def other_core(value):
    return permuted(value, lambda i, n: i ^ 1)


def other_column(value):
    return permuted(value, lambda i, n: i ^ 2)


def chip_up(value):
    return permuted(value, lambda i, n: (i + 4) % n)


def chip_down(value):
    return permuted(value, lambda i, n: (i - 4) % n)


def grid_gather(centroids):
    rows = centroids.shape[0] // CHUNKS
    levels = lax.axis_size("blk") // 4
    moving = [centroids[h * rows : (h + 1) * rows] for h in range(CHUNKS)]
    places = []
    for shift in range(levels):
        if shift:
            moving = [chip_up(v) for v in moving]
        across = [other_column(v) for v in moving]
        places += [moving, [other_core(v) for v in moving]]
        places += [across, [other_core(v) for v in across]]
    return places


def grid_place(panel, device):
    levels = lax.axis_size("blk") // 4
    shift = (device // 4 - panel // 4) % levels
    return shift * 4 + ((panel ^ device) & 3)


def packed(value):
    return (value * LINK_SCALE).astype(jnp.float16)


def grid_reduce(sums):
    levels = lax.axis_size("blk") // 4
    rows = sums.shape[1] // CHUNKS
    whole = []
    for h in range(CHUNKS):
        part = sums[:, h * rows : (h + 1) * rows] * LINK_SCALE

        def paired(place):
            return part[place] + other_core(part[place + 1].astype(jnp.float16)).astype(jnp.float32)

        total = None
        for shift in reversed(range(levels)):
            away = other_column(paired(shift * 4 + 2).astype(jnp.float16))
            here = paired(shift * 4) + away.astype(jnp.float32)
            if total is not None:
                here = here + chip_down(total.astype(jnp.float16)).astype(jnp.float32)
            total = here
        whole.append(total)
    return jnp.concatenate(whole) * (1.0 / LINK_SCALE)


def ring_gather(centroids):
    places = []
    for offset in range(-SPAN, SPAN + 1):
        piece = permuted(centroids, lambda i, n: (i - offset) % n) if offset else centroids
        rows = piece.shape[0] // CHUNKS
        places.append([piece[h * rows : (h + 1) * rows] for h in range(CHUNKS)])
    return places


def ring_place(panel, device):
    return (panel - device + SPAN) % lax.axis_size("blk")


def ring_reduce(sums):
    total = sums[SPAN]
    for offset in range(-SPAN, SPAN + 1):
        if offset:
            arrived = permuted(packed(sums[offset + SPAN]), lambda i, n: (i + offset) % n)
            total = total + arrived.astype(jnp.float32) * (1.0 / LINK_SCALE)
    return total


def kernel(places, pieces, slots_ref, rows_ref, *refs):
    piece_refs = refs[: places * pieces]
    logs_ref, sums_ref, totals_ref, panels, norms, logits, sem = refs[places * pieces :]
    step = pl.program_id(0)
    listed = logits.shape[0]
    piece_rows = panels.shape[1] // pieces

    @pl.when(step == 0)
    def _():
        copies = [
            pltpu.make_async_copy(
                piece_refs[p * pieces + h],
                panels.at[p, pl.ds(h * piece_rows, piece_rows)],
                sem.at[p * pieces + h],
            )
            for p in range(places)
            for h in range(pieces)
        ]
        for copy in copies:
            copy.start()
        sums_ref[...] = jnp.zeros_like(sums_ref)
        totals_ref[...] = jnp.zeros_like(totals_ref)
        for copy in copies:
            copy.wait()

        @pl.loop(0, places)
        def _(p):
            wide = panels[p].astype(jnp.float32)
            norm = jnp.sum(wide * wide, axis=1, keepdims=True)
            norms[p] = jnp.broadcast_to(norm * (0.5 * LOGIT_SCALE * LOG2E), norms.shape[1:])

    block = rows_ref[...]
    highest = None
    for l in range(listed):
        place = slots_ref[step * listed + l]
        scores = lax.dot_general(
            panels[place], block, (((1,), (1,)), ((), ())), preferred_element_type=jnp.float32
        )
        norm = norms[place]
        scores = scores * (LOGIT_SCALE * LOG2E) - jnp.concatenate([norm, norm], axis=1)
        logits[l] = scores
        top = jnp.max(scores, axis=0, keepdims=True)
        highest = top if highest is None else jnp.maximum(highest, top)
    mass = jnp.zeros_like(highest)
    for l in range(listed):
        powers = jnp.exp2(logits[l] - highest)
        logits[l] = powers
        mass = mass + jnp.sum(powers, axis=0, keepdims=True)
    logs_ref[0] = (highest + jnp.log2(mass)) * (1.0 / LOG2E)
    share = 1.0 / mass
    for l in range(listed):
        place = slots_ref[step * listed + l]
        weights = (logits[l] * share).astype(jnp.bfloat16)
        sums_ref[place] += jnp.dot(weights, block, preferred_element_type=jnp.float32)
        wide = weights.astype(jnp.float32)
        totals_ref[place] += wide[:, :128] + wide[:, 128:]


def scored_sums(pieces_of, rows, slots):
    places, pieces = len(pieces_of), len(pieces_of[0])
    width = rows.shape[1]
    blocks, listed = slots.shape
    cent = pieces_of[0][0].shape[0] * pieces
    flat = [piece for place in pieces_of for piece in place]
    flops = 4 * rows.shape[0] * listed * cent * width

    def body(*refs):
        kernel(places, pieces, *refs)

    logs, sums, totals = pl.pallas_call(
        body,
        out_shape=(
            jax.ShapeDtypeStruct((blocks, 1, BLOCK), jnp.float32),
            jax.ShapeDtypeStruct((places, cent, width), jnp.float32),
            jax.ShapeDtypeStruct((places, cent, 128), jnp.float32),
        ),
        grid_spec=pltpu.PrefetchScalarGridSpec(
            num_scalar_prefetch=1,
            grid=(blocks,),
            in_specs=[pl.BlockSpec((BLOCK, width), lambda b, s: (b, 0))]
            + [pl.BlockSpec(memory_space=pl.ANY)] * len(flat),
            out_specs=(
                pl.BlockSpec((1, 1, BLOCK), lambda b, s: (b, 0, 0)),
                pl.BlockSpec((places, cent, width), lambda b, s: (0, 0, 0), pipeline_mode=pl.Buffered(1)),
                pl.BlockSpec((places, cent, 128), lambda b, s: (0, 0, 0), pipeline_mode=pl.Buffered(1)),
            ),
            scratch_shapes=[
                pltpu.VMEM((places, cent, width), jnp.bfloat16),
                pltpu.VMEM((places, cent, 128), jnp.float32),
                pltpu.VMEM((listed, cent, BLOCK), jnp.float32),
                pltpu.SemaphoreType.DMA((places * pieces,)),
            ],
        ),
        compiler_params=pltpu.CompilerParams(
            dimension_semantics=("arbitrary",), vmem_limit_bytes=48 << 20
        ),
        cost_estimate=pl.CostEstimate(
            flops=flops,
            bytes_accessed=rows.size * 2 + places * cent * width * 6,
            transcendentals=rows.shape[0] * listed * cent,
        ),
        name="scored_sums",
    )(slots.reshape(-1), rows, *flat)
    return logs.reshape(-1), sums, jnp.sum(totals, axis=-1)


def on_device(rows, centroids, lists):
    count = lax.axis_size("blk")
    device = lax.axis_index("blk")
    on_grid = count == 16
    place_of = grid_place if on_grid else ring_place
    pieces_of = grid_gather(centroids) if on_grid else ring_gather(centroids)
    slots = place_of(lists, device).astype(jnp.int32)
    log_totals, sums, totals = scored_sums(pieces_of, rows, slots)
    everyone = jnp.arange(count, dtype=jnp.int32)
    places = place_of(everyone, device)
    used = places < len(pieces_of)
    by_panel = jnp.where(used[:, None], totals[jnp.where(used, places, 0)], 0.0)
    own_totals = lax.psum_scatter(by_panel.reshape(-1), "blk", tiled=True)
    own_sums = grid_reduce(sums) if on_grid else ring_reduce(sums)
    updated = (own_sums + PRIOR_MASS * centroids.astype(jnp.float32)) / (
        own_totals[:, None] + PRIOR_MASS
    )
    return updated, log_totals


def solution(mesh):
    placed = P(("groups", "blk"), None)
    return jax.shard_map(
        on_device,
        mesh=mesh,
        in_specs=(placed, placed, placed),
        out_specs=(placed, P(("groups", "blk"))),
        check_vma=False,
    )
```

time: 622 us -> 218 us (0.35)
  waiting for transfers between devices: 332 us -> 52.6 us
  matrix products: 168 us -> 0 us
  blocking collectives: 0 us -> 58.5 us
  Pallas kernels: 0 us -> 48.2 us
  local copies, waits for them, and re-layouts: 49.3 us -> 3.69 us
  starting transfers between devices: 55.5 us -> 42 us
    ppermute x39 -> x60, waiting for transfers between devices: 332 us -> 52.6 us  [permuted(): lax.ppermute(value, 'blk', [(i, target(i, count)) for i in range(count)])]
    dot_general x16 -> x0, matrix products: 168 us -> none  [the longest x4 128 us: score_group(): jnp.einsum('glw,glcd->wcd', slot_lookup_table, partial_value, precision=l...]
    unnamed x0 -> x1, blocking collectives: none -> 58.5 us
    pallas_call x0 -> x1, Pallas kernels: none -> 48.2 us  [scored_sums(): pl.pallas_call(body, out_shape=(jax.ShapeDtypeStruct((blocks, 1, BLOCK),...]
    gather x8 -> x1, local copies, waits for them, and re-layouts: 35.4 us -> 0.58 us  [on_device(): by_panel = jnp.where(used[:, None], totals[jnp.where(used, places, 0)], 0.0)]
    ppermute x39 -> x60, starting transfers between devices: 55.5 us -> 42 us  [permuted(): lax.ppermute(value, 'blk', [(i, target(i, count)) for i in range(count)])]
    while x1 -> x0, local copies, waits for them, and re-layouts: 10.5 us -> none  [on_device(): lax.scan(score_group, start, (grouped_rows, slot_groups))]
  transfers between devices with their start and end apart: 39 -> 60, of which waited for: 38 -> 23; matrix products, arithmetic and copies ran while one was open for 0% -> 2% of each run, Pallas kernels for 0% -> 0%
where the time goes in v1:
time: 218 us
  blocking collectives  58.5 us (27%)
  waiting for transfers between devices  52.6 us (24%)
  Pallas kernels  48.2 us (22%)
  starting transfers between devices  42 us (19%)
  other arithmetic  11.3 us (5%)
  local copies, waits for them, and re-layouts  3.69 us (2%)
    unnamed x1, blocking collectives  58.5 us
    ppermute x60, waiting for transfers between devices, permuted(): lax.ppermute(value, 'blk', [(i, target(i, count)) for i in range(count)])  52.6 us
    pallas_call x1, Pallas kernels, scored_sums(): pl.pallas_call(body, out_shape=(jax.ShapeDtypeStruct((blocks, 1, BLOCK),...  48.2 us
    ppermute x60, starting transfers between devices, permuted(): lax.ppermute(value, 'blk', [(i, target(i, count)) for i in range(count)])  42 us
    another operation x1, other arithmetic  5.69 us
  transfers between devices with their start and end apart: 60, of which 23 were waited for; matrix products, arithmetic and copies ran while one was open for 2% of the time, Pallas kernels for 0%

profile of v1, /device:TPU:0, one launch (start us, length us, event | category | flops | bytes accessed | tf_op | source)
XLA Modules:
  0.0 217.9 jit_solution(843454578029855681)
XLA Ops:
  1.7 3.1 %collective-permute-start.7 = (bf16[128,768]{1,0:T(8,128)(2,1)S(1)}, bf16[128,768]{1,0:T(8,128)(2,1)S(1)}, u32[]{:S(2)}, u32[]{:S(2)}) collective-permute-start(bf16[128,768]{1,0:T(8,128)(2,1)S(1)} %get-tuple-element.36.refs_3_), channel_id=1, source_target_pairs={{0,4},{1,5},{2,6},{3,7},{4,8},{5,9},{6,10},{7,11},{8,12},{9,13},{1... | collective-permute-start | bytes 589832 | tf_op jit(solution)/shard_map/ppermute | solution.py:21
  4.8 1.5 collective-permute-start.3
  6.3 1.6 collective-permute-start.6
  8.4 3.8 %collective-permute-done.7.refs_11_ = bf16[128,768]{1,0:T(8,128)(2,1)S(1)} collective-permute-done((bf16[128,768]{1,0:T(8,128)(2,1)S(1)}, bf16[128,768]{1,0:T(8,128)(2,1)S(1)}, u32[]{:S(2)}, u32[]{:S(2)}) %collective-permute-start.7) | collective-permute-done | bytes 196640 | tf_op jit(solution)/shard_map/ppermute | solution.py:21
  13.1 2.5 %collective-permute-start.11 = (bf16[128,768]{1,0:T(8,128)(2,1)S(1)}, bf16[128,768]{1,0:T(8,128)(2,1)S(1)}, u32[]{:S(2)}, u32[]{:S(2)}) collective-permute-start(bf16[128,768]{1,0:T(8,128)(2,1)S(1)} %collective-permute-done.7.refs_11_), channel_id=1, source_target_pairs={{0,2},{1,3},{2,0},{3,1},{4,6},{5,7},{6,4},{7,5},{8,10},{9,11},{10,... | collective-permute-start | bytes 589832 | tf_op jit(solution)/shard_map/ppermute | solution.py:21
  17.8 3.8 %collective-permute-done.15.refs_19_ = bf16[128,768]{1,0:T(8,128)(2,1)S(1)} collective-permute-done((bf16[128,768]{1,0:T(8,128)(2,1)S(1)}, bf16[128,768]{1,0:T(8,128)(2,1)S(1)}, u32[]{:S(2)}, u32[]{:S(2)}) %collective-permute-start.15) | collective-permute-done | bytes 196640 | tf_op jit(solution)/shard_map/ppermute | solution.py:21
  21.5 2.2 %collective-permute-start.10 = (bf16[128,768]{1,0:T(8,128)(2,1)S(1)}, bf16[128,768]{1,0:T(8,128)(2,1)S(1)}, u32[]{:S(2)}, u32[]{:S(2)}) collective-permute-start(bf16[128,768]{1,0:T(8,128)(2,1)S(1)} %collective-permute-done.6.refs_10_), channel_id=1, source_target_pairs={{0,2},{1,3},{2,0},{3,1},{4,6},{5,7},{6,4},{7,5},{8,10},{9,11},{10,... | collective-permute-start | bytes 589832 | tf_op jit(solution)/shard_map/ppermute | solution.py:21
  25.5 2.2 collective-permute-start.19
  28.7 4.3 %collective-permute-done.23.refs_27_ = bf16[128,768]{1,0:T(8,128)(2,1)S(1)} collective-permute-done((bf16[128,768]{1,0:T(8,128)(2,1)S(1)}, bf16[128,768]{1,0:T(8,128)(2,1)S(1)}, u32[]{:S(2)}, u32[]{:S(2)}) %collective-permute-start.23) | collective-permute-done | bytes 196640 | tf_op jit(solution)/shard_map/ppermute | solution.py:21
  33.5 2.0 collective-permute-start.27
  35.5 1.9 collective-permute-done.22.refs_26_
  37.5 3.4 %collective-permute-done.18.refs_22_ = bf16[128,768]{1,0:T(8,128)(2,1)} collective-permute-done((bf16[128,768]{1,0:T(8,128)(2,1)S(1)}, bf16[128,768]{1,0:T(8,128)(2,1)}, u32[]{:S(2)}, u32[]{:S(2)}) %collective-permute-start.18) | collective-permute-done | bytes 196640 | tf_op jit(solution)/shard_map/ppermute | solution.py:21
  45.7 1.9 collective-permute-done.26.refs_30_
  47.6 1.6 collective-permute-done.28.refs_32_
  49.2 48.2 %scored_sums.1 = (f32[16,1,256]{2,1,0:T(1,128)}, f32[16,256,768]{2,1,0:T(8,128)}, f32[16,256,128]{2,1,0:T(8,128)}) custom-call(s32[96]{0:T(128)S(1)} %reshape.135.refs_0_, bf16[4096,768]{1,0:T(8,128)(2,1)} %refs_1_.1, bf16[128,768]{1,0:T(8,128)(2,1)S(1)} %get-tuple-element.37.refs_2_, bf16[128,768]{1,0:T(8,128)(2,1)S(1)} %get-tuple-element.36.refs_3_, ...), custom_call_target="tpu_custom_call" | custom-call | flops 19327352832 | bytes 25165824 | tf_op jit(solution)/shard_map/scored_sums/pallas_call | solution.py:176
  97.4 2.2 %reduce_sum.9 = f32[16,256]{1,0:T(8,128)S(1)} reduce(f32[16,256,128]{2,1,0:T(8,128)} %get-tuple-element.6, f32[]{:T(128)} %constant.80.clone.1), dimensions={2}, to_apply=%region_0.1 | reduce | flops 520192 | bytes 2113540 | tf_op jit(solution)/shard_map/reduce_sum | solution.py:210
  100.3 58.5 %all-reduce = f32[4096]{0:T(1024)S(1)} all-reduce(f32[4096]{0:T(1024)S(1)} %bitcast.159), channel_id=2, replica_groups=mesh['groups'=2,'blk'=16] {'blk'}, use_global_device_ids=true, to_apply=%region_1.2.clone | all-reduce | flops 4096 | bytes 32768
  158.8 5.7 %fusion.62 = (f16[16,128,768]{2,1,0:T(8,128)(2,1)S(1)}, f16[16,128,768]{2,1,0:T(8,128)(2,1)S(1)}, f32[16,128,768]{2,1,0:T(8,128)S(1)}, f32[16,128,768]{2,1,0:T(8,128)S(1)}) fusion(f32[16,256,768]{2,1,0:T(8,128)} %get-tuple-element.5), kind=kLoop, calls=%fused_computation.125 | loop fusion | flops 6291456 | bytes 31457280 | tf_op jit(solution)/shard_map/convert.15
  169.1 6.0 %collective-permute-done.41 = f16[128,768]{1,0:T(8,128)(2,1)S(1)} collective-permute-done((f16[128,768]{1,0:T(8,128)(2,1)S(1)}, f16[128,768]{1,0:T(8,128)(2,1)S(1)}, u32[]{:S(2)}, u32[]{:S(2)}) %collective-permute-start.41) | collective-permute-done | bytes 196640 | tf_op jit(solution)/shard_map/ppermute | solution.py:21
  176.4 5.1 %collective-permute-done.56 = f16[128,768]{1,0:T(8,128)(2,1)S(1)} collective-permute-done((f16[128,768]{1,0:T(8,128)(2,1)S(1)}, f16[128,768]{1,0:T(8,128)(2,1)S(1)}, u32[]{:S(2)}, u32[]{:S(2)}) %collective-permute-start.56) | collective-permute-done | bytes 196640 | tf_op jit(solution)/shard_map/ppermute | solution.py:21
  183.6 2.1 collective-permute-start.57
  185.7 1.5 collective-permute-done.38
  187.9 2.1 collective-permute-done.57
  190.1 1.7 collective-permute-start.35
  191.8 2.4 %collective-permute-done.53 = f16[128,768]{1,0:T(8,128)(2,1)S(1)} collective-permute-done((f16[128,768]{1,0:T(8,128)(2,1)S(1)}, f16[128,768]{1,0:T(8,128)(2,1)S(1)}, u32[]{:S(2)}, u32[]{:S(2)}) %collective-permute-start.53) | collective-permute-done | bytes 196640 | tf_op jit(solution)/shard_map/ppermute | solution.py:21
  194.3 1.6 collective-permute-start.43
  198.0 2.3 %collective-permute-done.43 = f16[128,768]{1,0:T(8,128)(2,1)S(1)} collective-permute-done((f16[128,768]{1,0:T(8,128)(2,1)S(1)}, f16[128,768]{1,0:T(8,128)(2,1)S(1)}, u32[]{:S(2)}, u32[]{:S(2)}) %collective-permute-start.43) | collective-permute-done | bytes 196640 | tf_op jit(solution)/shard_map/ppermute | solution.py:21
  200.3 3.1 %collective-permute-start.58 = (f16[128,768]{1,0:T(8,128)(2,1)S(1)}, f16[128,768]{1,0:T(8,128)(2,1)S(1)}, u32[]{:S(2)}, u32[]{:S(2)}) collective-permute-start(f16[128,768]{1,0:T(8,128)(2,1)S(1)} %fusion.12), channel_id=1, source_target_pairs={{0,12},{1,13},{2,14},{3,15},{4,0},{5,1},{6,2},{7,3},{8,4},{9,5},{1... | collective-permute-start | bytes 589832 | tf_op jit(solution)/shard_map/ppermute | solution.py:21
  203.8 1.7 collective-permute-start.47
  206.6 4.3 %collective-permute-start.44 = (f16[128,768]{1,0:T(8,128)(2,1)S(1)}, f16[128,768]{1,0:T(8,128)(2,1)S(1)}, u32[]{:S(2)}, u32[]{:S(2)}) collective-permute-start(f16[128,768]{1,0:T(8,128)(2,1)S(1)} %fusion.40), channel_id=1, source_target_pairs={{0,12},{1,13},{2,14},{3,15},{4,0},{5,1},{6,2},{7,3},{8,4},{9,5},{1... | collective-permute-start | bytes 589832 | tf_op jit(solution)/shard_map/ppermute | solution.py:21
  211.1 3.0 %collective-permute-done.44 = f16[128,768]{1,0:T(8,128)(2,1)S(1)} collective-permute-done((f16[128,768]{1,0:T(8,128)(2,1)S(1)}, f16[128,768]{1,0:T(8,128)(2,1)S(1)}, u32[]{:S(2)}, u32[]{:S(2)}) %collective-permute-start.44) | collective-permute-done | bytes 196640 | tf_op jit(solution)/shard_map/ppermute | solution.py:21
  214.1 2.5 %collective-permute-done.59 = f16[128,768]{1,0:T(8,128)(2,1)S(1)} collective-permute-done((f16[128,768]{1,0:T(8,128)(2,1)S(1)}, f16[128,768]{1,0:T(8,128)(2,1)S(1)}, u32[]{:S(2)}, u32[]{:S(2)}) %collective-permute-start.59) | collective-permute-done | bytes 196640 | tf_op jit(solution)/shard_map/ppermute | solution.py:21
  (121 shorter events, 26.5 us)
Async XLA Ops:
  1.7 10.4 %collective-permute-start.7 = (bf16[128,768]{1,0:T(8,128)(2,1)S(1)}, bf16[128,768]{1,0:T(8,128)(2,1)S(1)}, u32[]{:S(2)}, u32[]{:S(2)}) collective-permute-start(bf16[128,768]{1,0:T(8,128)(2,1)S(1)} %get-tuple-element.36.refs_3_), channel_id=1, source_target_pairs={{0,4},{1,5},{2,6},{3,7},{4,8},{5,9},{6,10},{7,11},{8,12},{9,13},{1... | collective-permute-start | bytes 589832 | tf_op jit(solution)/shard_map/ppermute | solution.py:21
  4.8 7.4 %collective-permute-start.3 = (bf16[128,768]{1,0:T(8,128)(2,1)S(1)}, bf16[128,768]{1,0:T(8,128)(2,1)S(1)}, u32[]{:S(2)}, u32[]{:S(2)}) collective-permute-start(bf16[128,768]{1,0:T(8,128)(2,1)S(1)} %get-tuple-element.36.refs_3_), channel_id=1, source_target_pairs={{0,2},{1,3},{2,0},{3,1},{4,6},{5,7},{6,4},{7,5},{8,10},{9,11},{10,... | collective-permute-start | bytes 589832 | tf_op jit(solution)/shard_map/ppermute | solution.py:21
  6.3 9.6 %collective-permute-start.6 = (bf16[128,768]{1,0:T(8,128)(2,1)S(1)}, bf16[128,768]{1,0:T(8,128)(2,1)S(1)}, u32[]{:S(2)}, u32[]{:S(2)}) collective-permute-start(bf16[128,768]{1,0:T(8,128)(2,1)S(1)} %get-tuple-element.37.refs_2_), channel_id=1, source_target_pairs={{0,4},{1,5},{2,6},{3,7},{4,8},{5,9},{6,10},{7,11},{8,12},{9,13},{1... | collective-permute-start | bytes 589832 | tf_op jit(solution)/shard_map/ppermute | solution.py:21
  7.9 8.0 %collective-permute-start.2 = (bf16[128,768]{1,0:T(8,128)(2,1)S(1)}, bf16[128,768]{1,0:T(8,128)(2,1)S(1)}, u32[]{:S(2)}, u32[]{:S(2)}) collective-permute-start(bf16[128,768]{1,0:T(8,128)(2,1)S(1)} %get-tuple-element.37.refs_2_), channel_id=1, source_target_pairs={{0,2},{1,3},{2,0},{3,1},{4,6},{5,7},{6,4},{7,5},{8,10},{9,11},{10,... | collective-permute-start | bytes 589832 | tf_op jit(solution)/shard_map/ppermute | solution.py:21
  12.1 9.4 %collective-permute-start.15 = (bf16[128,768]{1,0:T(8,128)(2,1)S(1)}, bf16[128,768]{1,0:T(8,128)(2,1)S(1)}, u32[]{:S(2)}, u32[]{:S(2)}) collective-permute-start(bf16[128,768]{1,0:T(8,128)(2,1)S(1)} %collective-permute-done.7.refs_11_), channel_id=1, source_target_pairs={{0,4},{1,5},{2,6},{3,7},{4,8},{5,9},{6,10},{7,11},{8,12},{9,13},{1... | collective-permute-start | bytes 589832 | tf_op jit(solution)/shard_map/ppermute | solution.py:21
  13.1 10.6 %collective-permute-start.11 = (bf16[128,768]{1,0:T(8,128)(2,1)S(1)}, bf16[128,768]{1,0:T(8,128)(2,1)S(1)}, u32[]{:S(2)}, u32[]{:S(2)}) collective-permute-start(bf16[128,768]{1,0:T(8,128)(2,1)S(1)} %collective-permute-done.7.refs_11_), channel_id=1, source_target_pairs={{0,2},{1,3},{2,0},{3,1},{4,6},{5,7},{6,4},{7,5},{8,10},{9,11},{10,... | collective-permute-start | bytes 589832 | tf_op jit(solution)/shard_map/ppermute | solution.py:21
  15.9 7.9 %collective-permute-start.9 = (bf16[128,768]{1,0:T(8,128)(2,1)S(1)}, bf16[128,768]{1,0:T(8,128)(2,1)S(1)}, u32[]{:S(2)}, u32[]{:S(2)}) collective-permute-start(bf16[128,768]{1,0:T(8,128)(2,1)S(1)} %collective-permute-done.7.refs_11_), channel_id=1, source_target_pairs={{0,1},{1,0},{2,3},{3,2},{4,5},{5,4},{6,7},{7,6},{8,9},{9,8},{10,11... | collective-permute-start | bytes 589832 | tf_op jit(solution)/shard_map/ppermute | solution.py:21
  15.9 8.4 %collective-permute-start.5 = (bf16[128,768]{1,0:T(8,128)(2,1)S(1)}, bf16[128,768]{1,0:T(8,128)(2,1)S(1)}, u32[]{:S(2)}, u32[]{:S(2)}) collective-permute-start(bf16[128,768]{1,0:T(8,128)(2,1)S(1)} %collective-permute-done.3.refs_7_), channel_id=1, source_target_pairs={{0,1},{1,0},{2,3},{3,2},{4,5},{5,4},{6,7},{7,6},{8,9},{9,8},{10,11... | collective-permute-start | bytes 589832 | tf_op jit(solution)/shard_map/ppermute | solution.py:21
  16.4 9.0 %collective-permute-start.14 = (bf16[128,768]{1,0:T(8,128)(2,1)S(1)}, bf16[128,768]{1,0:T(8,128)(2,1)S(1)}, u32[]{:S(2)}, u32[]{:S(2)}) collective-permute-start(bf16[128,768]{1,0:T(8,128)(2,1)S(1)} %collective-permute-done.6.refs_10_), channel_id=1, source_target_pairs={{0,4},{1,5},{2,6},{3,7},{4,8},{5,9},{6,10},{7,11},{8,12},{9,13},{1... | collective-permute-start | bytes 589832 | tf_op jit(solution)/shard_map/ppermute | solution.py:21
  24.3 8.7 %collective-permute-start.23 = (bf16[128,768]{1,0:T(8,128)(2,1)S(1)}, bf16[128,768]{1,0:T(8,128)(2,1)S(1)}, u32[]{:S(2)}, u32[]{:S(2)}) collective-permute-start(bf16[128,768]{1,0:T(8,128)(2,1)S(1)} %collective-permute-done.15.refs_19_), channel_id=1, source_target_pairs={{0,4},{1,5},{2,6},{3,7},{4,8},{5,9},{6,10},{7,11},{8,12},{9,13},{1... | collective-permute-start | bytes 589832 | tf_op jit(solution)/shard_map/ppermute | solution.py:21
  25.5 7.5 %collective-permute-start.19 = (bf16[128,768]{1,0:T(8,128)(2,1)S(1)}, bf16[128,768]{1,0:T(8,128)(2,1)S(1)}, u32[]{:S(2)}, u32[]{:S(2)}) collective-permute-start(bf16[128,768]{1,0:T(8,128)(2,1)S(1)} %collective-permute-done.15.refs_19_), channel_id=1, source_target_pairs={{0,2},{1,3},{2,0},{3,1},{4,6},{5,7},{6,4},{7,5},{8,10},{9,11},{10,... | collective-permute-start | bytes 589832 | tf_op jit(solution)/shard_map/ppermute | solution.py:21
  28.7 8.8 %collective-permute-start.22 = (bf16[128,768]{1,0:T(8,128)(2,1)S(1)}, bf16[128,768]{1,0:T(8,128)(2,1)}, u32[]{:S(2)}, u32[]{:S(2)}) collective-permute-start(bf16[128,768]{1,0:T(8,128)(2,1)S(1)} %collective-permute-done.14.refs_18_), channel_id=1, source_target_pairs={{0,4},{1,5},{2,6},{3,7},{4,8},{5,9},{6,10},{7,11},{8,12},{9,13},{1... | collective-permute-start | bytes 589832 | tf_op jit(solution)/shard_map/ppermute | solution.py:21
  33.0 7.9 %collective-permute-start.18 = (bf16[128,768]{1,0:T(8,128)(2,1)S(1)}, bf16[128,768]{1,0:T(8,128)(2,1)}, u32[]{:S(2)}, u32[]{:S(2)}) collective-permute-start(bf16[128,768]{1,0:T(8,128)(2,1)S(1)} %collective-permute-done.14.refs_18_), channel_id=1, source_target_pairs={{0,2},{1,3},{2,0},{3,1},{4,6},{5,7},{6,4},{7,5},{8,10},{9,11},{10,... | collective-permute-start | bytes 589832 | tf_op jit(solution)/shard_map/ppermute | solution.py:21
  33.0 10.7 %collective-permute-start.16 = (bf16[128,768]{1,0:T(8,128)(2,1)S(1)}, bf16[128,768]{1,0:T(8,128)(2,1)}, u32[]{:S(2)}, u32[]{:S(2)}) collective-permute-start(bf16[128,768]{1,0:T(8,128)(2,1)S(1)} %collective-permute-done.14.refs_18_), channel_id=1, source_target_pairs={{0,1},{1,0},{2,3},{3,2},{4,5},{5,4},{6,7},{7,6},{8,9},{9,8},{10,11... | collective-permute-start | bytes 589832 | tf_op jit(solution)/shard_map/ppermute | solution.py:21
  33.0 10.8 %collective-permute-start.12 = (bf16[128,768]{1,0:T(8,128)(2,1)S(1)}, bf16[128,768]{1,0:T(8,128)(2,1)}, u32[]{:S(2)}, u32[]{:S(2)}) collective-permute-start(bf16[128,768]{1,0:T(8,128)(2,1)S(1)} %collective-permute-done.10.refs_14_), channel_id=1, source_target_pairs={{0,1},{1,0},{2,3},{3,2},{4,5},{5,4},{6,7},{7,6},{8,9},{9,8},{10,11... | collective-permute-start | bytes 589832 | tf_op jit(solution)/shard_map/ppermute | solution.py:21
  33.5 11.6 %collective-permute-start.27 = (bf16[128,768]{1,0:T(8,128)(2,1)S(1)}, bf16[128,768]{1,0:T(8,128)(2,1)}, u32[]{:S(2)}, u32[]{:S(2)}) collective-permute-start(bf16[128,768]{1,0:T(8,128)(2,1)S(1)} %collective-permute-done.23.refs_27_), channel_id=1, source_target_pairs={{0,2},{1,3},{2,0},{3,1},{4,6},{5,7},{6,4},{7,5},{8,10},{9,11},{10,... | collective-permute-start | bytes 589832 | tf_op jit(solution)/shard_map/ppermute | solution.py:21
  37.5 7.7 %collective-permute-start.25 = (bf16[128,768]{1,0:T(8,128)(2,1)S(1)}, bf16[128,768]{1,0:T(8,128)(2,1)}, u32[]{:S(2)}, u32[]{:S(2)}) collective-permute-start(bf16[128,768]{1,0:T(8,128)(2,1)S(1)} %collective-permute-done.23.refs_27_), channel_id=1, source_target_pairs={{0,1},{1,0},{2,3},{3,2},{4,5},{5,4},{6,7},{7,6},{8,9},{9,8},{10,11... | collective-permute-start | bytes 589832 | tf_op jit(solution)/shard_map/ppermute | solution.py:21
  167.9 7.2 %collective-permute-start.41 = (f16[128,768]{1,0:T(8,128)(2,1)S(1)}, f16[128,768]{1,0:T(8,128)(2,1)S(1)}, u32[]{:S(2)}, u32[]{:S(2)}) collective-permute-start(f16[128,768]{1,0:T(8,128)(2,1)S(1)} %fusion.25), channel_id=1, source_target_pairs={{0,2},{1,3},{2,0},{3,1},{4,6},{5,7},{6,4},{7,5},{8,10},{9,11},{10,... | collective-permute-start | bytes 589832 | tf_op jit(solution)/shard_map/ppermute | solution.py:21
  168.0 7.7 %collective-permute-start.54 = (f16[128,768]{1,0:T(8,128)(2,1)S(1)}, f16[128,768]{1,0:T(8,128)(2,1)S(1)}, u32[]{:S(2)}, u32[]{:S(2)}) collective-permute-start(f16[128,768]{1,0:T(8,128)(2,1)S(1)} %get-tuple-element.30), channel_id=1, source_target_pairs={{0,1},{1,0},{2,3},{3,2},{4,5},{5,4},{6,7},{7,6},{8,9},{9,8},{10,11... | collective-permute-start | bytes 589832 | tf_op jit(solution)/shard_map/ppermute | solution.py:21
  168.5 7.3 %collective-permute-start.52 = (f16[128,768]{1,0:T(8,128)(2,1)S(1)}, f16[128,768]{1,0:T(8,128)(2,1)S(1)}, u32[]{:S(2)}, u32[]{:S(2)}) collective-permute-start(f16[128,768]{1,0:T(8,128)(2,1)S(1)} %get-tuple-element.31), channel_id=1, source_target_pairs={{0,1},{1,0},{2,3},{3,2},{4,5},{5,4},{6,7},{7,6},{8,9},{9,8},{10,11... | collective-permute-start | bytes 589832 | tf_op jit(solution)/shard_map/ppermute | solution.py:21
  168.6 7.7 %collective-permute-start.49 = (f16[128,768]{1,0:T(8,128)(2,1)S(1)}, f16[128,768]{1,0:T(8,128)(2,1)S(1)}, u32[]{:S(2)}, u32[]{:S(2)}) collective-permute-start(f16[128,768]{1,0:T(8,128)(2,1)S(1)} %get-tuple-element.33), channel_id=1, source_target_pairs={{0,1},{1,0},{2,3},{3,2},{4,5},{5,4},{6,7},{7,6},{8,9},{9,8},{10,11... | collective-permute-start | bytes 589832 | tf_op jit(solution)/shard_map/ppermute | solution.py:21
  169.0 7.4 %collective-permute-start.46 = (f16[128,768]{1,0:T(8,128)(2,1)S(1)}, f16[128,768]{1,0:T(8,128)(2,1)S(1)}, u32[]{:S(2)}, u32[]{:S(2)}) collective-permute-start(f16[128,768]{1,0:T(8,128)(2,1)S(1)} %get-tuple-element.35), channel_id=1, source_target_pairs={{0,1},{1,0},{2,3},{3,2},{4,5},{5,4},{6,7},{7,6},{8,9},{9,8},{10,11... | collective-permute-start | bytes 589832 | tf_op jit(solution)/shard_map/ppermute | solution.py:21
  175.7 35.3 %collective-permute-start.30 = (f16[128,768]{1,0:T(8,128)(2,1)S(1)}, f16[128,768]{1,0:T(8,128)(2,1)S(1)}, u32[]{:S(2)}, u32[]{:S(2)}) collective-permute-start(f16[128,768]{1,0:T(8,128)(2,1)S(1)} %get-tuple-element.20), channel_id=1, source_target_pairs={{0,1},{1,0},{2,3},{3,2},{4,5},{5,4},{6,7},{7,6},{8,9},{9,8},{10,11... | collective-permute-start | bytes 589832 | tf_op jit(solution)/shard_map/ppermute | solution.py:21
  176.3 19.7 %collective-permute-start.33 = (f16[128,768]{1,0:T(8,128)(2,1)S(1)}, f16[128,768]{1,0:T(8,128)(2,1)S(1)}, u32[]{:S(2)}, u32[]{:S(2)}) collective-permute-start(f16[128,768]{1,0:T(8,128)(2,1)S(1)} %get-tuple-element.26), channel_id=1, source_target_pairs={{0,1},{1,0},{2,3},{3,2},{4,5},{5,4},{6,7},{7,6},{8,9},{9,8},{10,11... | collective-permute-start | bytes 589832 | tf_op jit(solution)/shard_map/ppermute | solution.py:21
  176.4 7.2 %collective-permute-start.42 = (f16[128,768]{1,0:T(8,128)(2,1)S(1)}, f16[128,768]{1,0:T(8,128)(2,1)S(1)}, u32[]{:S(2)}, u32[]{:S(2)}) collective-permute-start(f16[128,768]{1,0:T(8,128)(2,1)S(1)} %get-tuple-element.13), channel_id=1, source_target_pairs={{0,12},{1,13},{2,14},{3,15},{4,0},{5,1},{6,2},{7,3},{8,4},{9,5},{1... | collective-permute-start | bytes 589832 | tf_op jit(solution)/shard_map/ppermute | solution.py:21
  187.2 7.1 %collective-permute-start.53 = (f16[128,768]{1,0:T(8,128)(2,1)S(1)}, f16[128,768]{1,0:T(8,128)(2,1)S(1)}, u32[]{:S(2)}, u32[]{:S(2)}) collective-permute-start(f16[128,768]{1,0:T(8,128)(2,1)S(1)} %get-tuple-element.18), channel_id=1, source_target_pairs={{0,2},{1,3},{2,0},{3,1},{4,6},{5,7},{6,4},{7,5},{8,10},{9,11},{10,... | collective-permute-start | bytes 589832 | tf_op jit(solution)/shard_map/ppermute | solution.py:21
  187.9 26.3 %collective-permute-start.45 = (f16[128,768]{1,0:T(8,128)(2,1)S(1)}, f16[128,768]{1,0:T(8,128)(2,1)S(1)}, u32[]{:S(2)}, u32[]{:S(2)}) collective-permute-start(f16[128,768]{1,0:T(8,128)(2,1)S(1)} %get-tuple-element.28), channel_id=1, source_target_pairs={{0,1},{1,0},{2,3},{3,2},{4,5},{5,4},{6,7},{7,6},{8,9},{9,8},{10,11... | collective-permute-start | bytes 589832 | tf_op jit(solution)/shard_map/ppermute | solution.py:21
  190.1 7.0 %collective-permute-start.35 = (f16[128,768]{1,0:T(8,128)(2,1)S(1)}, f16[128,768]{1,0:T(8,128)(2,1)S(1)}, u32[]{:S(2)}, u32[]{:S(2)}) collective-permute-start(f16[128,768]{1,0:T(8,128)(2,1)S(1)} %get-tuple-element.15), channel_id=1, source_target_pairs={{0,2},{1,3},{2,0},{3,1},{4,6},{5,7},{6,4},{7,5},{8,10},{9,11},{10,... | collective-permute-start | bytes 589832 | tf_op jit(solution)/shard_map/ppermute | solution.py:21
  196.0 7.5 %collective-permute-start.48 = (f16[128,768]{1,0:T(8,128)(2,1)S(1)}, f16[128,768]{1,0:T(8,128)(2,1)S(1)}, u32[]{:S(2)}, u32[]{:S(2)}) collective-permute-start(f16[128,768]{1,0:T(8,128)(2,1)S(1)} %get-tuple-element.34), channel_id=1, source_target_pairs={{0,1},{1,0},{2,3},{3,2},{4,5},{5,4},{6,7},{7,6},{8,9},{9,8},{10,11... | collective-permute-start | bytes 589832 | tf_op jit(solution)/shard_map/ppermute | solution.py:21
  203.5 7.5 %collective-permute-start.32 = (f16[128,768]{1,0:T(8,128)(2,1)S(1)}, f16[128,768]{1,0:T(8,128)(2,1)S(1)}, u32[]{:S(2)}, u32[]{:S(2)}) collective-permute-start(f16[128,768]{1,0:T(8,128)(2,1)S(1)} %get-tuple-element.12), channel_id=1, source_target_pairs={{0,2},{1,3},{2,0},{3,1},{4,6},{5,7},{6,4},{7,5},{8,10},{9,11},{10,... | collective-permute-start | bytes 589832 | tf_op jit(solution)/shard_map/ppermute | solution.py:21
  203.8 10.3 %collective-permute-start.47 = (f16[128,768]{1,0:T(8,128)(2,1)S(1)}, f16[128,768]{1,0:T(8,128)(2,1)S(1)}, u32[]{:S(2)}, u32[]{:S(2)}) collective-permute-start(f16[128,768]{1,0:T(8,128)(2,1)S(1)} %get-tuple-element.16), channel_id=1, source_target_pairs={{0,2},{1,3},{2,0},{3,1},{4,6},{5,7},{6,4},{7,5},{8,10},{9,11},{10,... | collective-permute-start | bytes 589832 | tf_op jit(solution)/shard_map/ppermute | solution.py:21
  206.6 7.5 %collective-permute-start.44 = (f16[128,768]{1,0:T(8,128)(2,1)S(1)}, f16[128,768]{1,0:T(8,128)(2,1)S(1)}, u32[]{:S(2)}, u32[]{:S(2)}) collective-permute-start(f16[128,768]{1,0:T(8,128)(2,1)S(1)} %fusion.40), channel_id=1, source_target_pairs={{0,12},{1,13},{2,14},{3,15},{4,0},{5,1},{6,2},{7,3},{8,4},{9,5},{1... | collective-permute-start | bytes 589832 | tf_op jit(solution)/shard_map/ppermute | solution.py:21
  (30 other events, 178.4 us)

commit v2 on v1

v2 whole, which is shorter than its diff:
```python
import math

import jax
import jax.numpy as jnp
from jax import lax
from jax.experimental import pallas as pl
from jax.experimental.pallas import tpu as pltpu
from jax.sharding import PartitionSpec as P

BLOCK = 256
SPAN = 6
LOGIT_SCALE = 0.25
PRIOR_MASS = 8.0
LOG2E = math.log2(math.e)
LINK_SCALE = 1.0 / 16.0
EXTRA = 8


def grid_plan(count):
    up = 4
    return 0, ((2, 0, up), (1, 0, None), (6, 0, -up), (3, 2, None), (7, 6, None), (5, 3, up))


def ring_plan(count):
    reach = (SPAN + 1) // 2
    steps = []
    for hop in range(reach):
        steps.append((reach + hop + 1, reach + hop, 2))
        steps.append((reach - hop - 1, reach - hop, -2))
    return reach, tuple(steps)


def plan_of(count):
    return grid_plan(count) if count == 16 else ring_plan(count)


def chip_place(panel, device, count):
    if count == 16:
        return (device // 4 - panel // 4) % 4 * 2 + ((panel ^ device) >> 1 & 1)
    chips = count // 2
    return (device // 2 - panel // 2 + (SPAN + 1) // 2) % chips


def moved(value, shift):
    count = lax.axis_size("blk")
    if shift is None:
        return lax.ppermute(value, "blk", [(i, i ^ 2) for i in range(count)])
    return lax.ppermute(value, "blk", [(i, (i + shift) % count) for i in range(count)])


def other_core(value):
    count = lax.axis_size("blk")
    return lax.ppermute(value, "blk", [(i, i ^ 1) for i in range(count)])


def gathered(centroids):
    own, steps = plan_of(lax.axis_size("blk"))
    here = {own: centroids}
    for place, source, shift in steps:
        here[place] = moved(here[source], shift)
    return here, {place: other_core(value) for place, value in here.items()}


def reduced(near, far):
    own, steps = plan_of(lax.axis_size("blk"))
    order = [place for place, _, _ in reversed(steps)] + [own]
    total = {place: (near[place] + other_core(far[place])) * LINK_SCALE for place in order}
    for place, source, shift in reversed(steps):
        back = moved(total[place].astype(jnp.float16), shift if shift is None else -shift)
        total[source] = total[source] + back.astype(jnp.float32)
    return total[own] * (1.0 / LINK_SCALE)


def kernel(places, slots_ref, rows_ref, *refs):
    count = len(places)
    near_refs, far_refs = refs[:count], refs[count : 2 * count]
    logs_ref, near_ref, far_ref, panels, norms, logits, totals, sem = refs[2 * count :]
    step = pl.program_id(0)
    listed = logits.shape[0]
    cent = panels.shape[1]

    @pl.when(step == 0)
    def _():
        copies = []
        for core, piece_refs in enumerate((near_refs, far_refs)):
            for at, ref in zip(places, piece_refs):
                copies.append(pltpu.make_async_copy(ref, panels.at[2 * at + core], sem.at[2 * at + core]))
        for copy in copies:
            copy.start()
        near_ref[...] = jnp.zeros_like(near_ref)
        far_ref[...] = jnp.zeros_like(far_ref)
        totals[...] = jnp.zeros_like(totals)
        for copy in copies:
            copy.wait()

        for at in places:

            @pl.loop(2 * at, 2 * at + 2)
            def _(p):
                wide = panels[p].astype(jnp.float32)
                norm = jnp.sum(wide * wide, axis=1, keepdims=True)
                norms[p] = jnp.broadcast_to(norm * (0.5 * LOGIT_SCALE * LOG2E), norms.shape[1:])

    block = rows_ref[...]
    highest = None
    for l in range(listed):
        place = slots_ref[step * listed + l]
        scores = lax.dot_general(
            panels[place], block, (((1,), (1,)), ((), ())), preferred_element_type=jnp.float32
        )
        norm = norms[place]
        scores = scores * (LOGIT_SCALE * LOG2E) - jnp.concatenate([norm, norm], axis=1)
        logits[l] = scores
        top = jnp.max(scores, axis=0, keepdims=True)
        highest = top if highest is None else jnp.maximum(highest, top)
    mass = jnp.zeros_like(highest)
    for l in range(listed):
        powers = jnp.exp2(logits[l] - highest)
        logits[l] = powers
        mass = mass + jnp.sum(powers, axis=0, keepdims=True)
    logs_ref[0] = (highest + jnp.log2(mass)) * (1.0 / LOG2E)
    share = 1.0 / mass
    for l in range(listed):
        place = slots_ref[step * listed + l]
        weights = (logits[l] * share).astype(jnp.bfloat16)
        partial = jnp.dot(weights, block, preferred_element_type=jnp.float32)
        wide = weights.astype(jnp.float32)
        totals[place] += wide[:, :128] + wide[:, 128:]

        @pl.when(place & 1 == 0)
        def _():
            near_ref[place >> 1, pl.ds(0, cent)] += partial

        @pl.when(place & 1 == 1)
        def _():
            far_ref[place >> 1, pl.ds(0, cent)] += partial

    @pl.when(step == pl.num_programs(0) - 1)
    def _():
        for at in places:
            for core, ref in enumerate((near_ref, far_ref)):
                row = jnp.sum(totals[2 * at + core].T, axis=0, keepdims=True)
                ref[at, pl.ds(cent, EXTRA), pl.ds(0, cent)] = jnp.broadcast_to(row, (EXTRA, cent))


def scored_sums(near, far, rows, slots):
    places = tuple(near)
    room = max(places) + 1
    width = rows.shape[1]
    blocks, listed = slots.shape
    cent = near[places[0]].shape[0]
    pieces = [near[p] for p in places] + [far[p] for p in places]
    whole = pl.BlockSpec((room, cent + EXTRA, width), lambda b, s: (0, 0, 0), pipeline_mode=pl.Buffered(1))

    def body(*refs):
        kernel(places, *refs)

    logs, near_sums, far_sums = pl.pallas_call(
        body,
        out_shape=(
            jax.ShapeDtypeStruct((blocks, 1, BLOCK), jnp.float32),
            jax.ShapeDtypeStruct((room, cent + EXTRA, width), jnp.float32),
            jax.ShapeDtypeStruct((room, cent + EXTRA, width), jnp.float32),
        ),
        grid_spec=pltpu.PrefetchScalarGridSpec(
            num_scalar_prefetch=1,
            grid=(blocks,),
            in_specs=[pl.BlockSpec((BLOCK, width), lambda b, s: (b, 0))]
            + [pl.BlockSpec(memory_space=pl.ANY)] * len(pieces),
            out_specs=(pl.BlockSpec((1, 1, BLOCK), lambda b, s: (b, 0, 0)), whole, whole),
            scratch_shapes=[
                pltpu.VMEM((2 * room, cent, width), jnp.bfloat16),
                pltpu.VMEM((2 * room, cent, 128), jnp.float32),
                pltpu.VMEM((listed, cent, BLOCK), jnp.float32),
                pltpu.VMEM((2 * room, cent, 128), jnp.float32),
                pltpu.SemaphoreType.DMA((2 * room,)),
            ],
        ),
        compiler_params=pltpu.CompilerParams(
            dimension_semantics=("arbitrary",), vmem_limit_bytes=48 << 20
        ),
        cost_estimate=pl.CostEstimate(
            flops=4 * rows.shape[0] * listed * cent * width,
            bytes_accessed=rows.size * 2 + len(pieces) * cent * width * 6,
            transcendentals=rows.shape[0] * listed * cent,
        ),
        name="scored_sums",
    )(slots.reshape(-1), rows, *pieces)
    return (
        logs.reshape(-1),
        {p: near_sums[p] for p in places},
        {p: far_sums[p] for p in places},
    )


def on_device(rows, centroids, lists):
    count = lax.axis_size("blk")
    device = lax.axis_index("blk")
    cent = centroids.shape[0]
    slots = 2 * chip_place(lists, device, count) + ((lists ^ device) & 1)
    near, far = gathered(centroids)
    log_totals, near_sums, far_sums = scored_sums(near, far, rows, slots.astype(jnp.int32))
    own = reduced(near_sums, far_sums)
    updated = (own[:cent] + PRIOR_MASS * centroids.astype(jnp.float32)) / (
        own[cent, :cent][:, None] + PRIOR_MASS
    )
    return updated, log_totals


def solution(mesh):
    placed = P(("groups", "blk"), None)
    return jax.shard_map(
        on_device,
        mesh=mesh,
        in_specs=(placed, placed, placed),
        out_specs=(placed, P(("groups", "blk"))),
        check_vma=False,
    )
```

time: 218 us -> 172 us (0.79)
  blocking collectives: 58.5 us -> 0 us
  waiting for transfers between devices: 52.6 us -> 70.5 us
  Pallas kernels: 48.2 us -> 65.9 us
  starting transfers between devices: 42 us -> 27.4 us
  other arithmetic: 11.3 us -> 2.93 us
    unnamed x1 -> x0, blocking collectives: 58.5 us -> none
    ppermute x60 -> x26, waiting for transfers between devices: 52.6 us -> 70.5 us  [the longest x6 37.3 us: moved(): return lax.ppermute(value, 'blk', [(i, i ^ 2) for i in range(count)])]
    pallas_call x1, Pallas kernels: 48.2 us -> 65.9 us  [scored_sums(): pl.pallas_call(body, out_shape=(jax.ShapeDtypeStruct((blocks, 1, BLOCK),...]
    ppermute x60 -> x26, starting transfers between devices: 42 us -> 27.4 us  [the longest x6 17.8 us: moved(): lax.ppermute(value, 'blk', [(i, (i + shift) % count) for i in range(count)])]
    another operation x1 -> x0, other arithmetic: 5.69 us -> none
    squeeze x0 -> x1, local copies, waits for them, and re-layouts: none -> 3.27 us  [scored_sums(): far_sums[p]]
    reduce_sum x1 -> x0, other arithmetic: 2.2 us -> none  [scored_sums(): return (logs.reshape(-1), sums, jnp.sum(totals, axis=-1))]
  transfers between devices with their start and end apart: 60 -> 26, of which waited for: 23 -> 15; matrix products, arithmetic and copies ran while one was open for 2% -> 1% of each run, Pallas kernels for 0% -> 0%
where the time goes in v2:
time: 172 us
  waiting for transfers between devices  70.5 us (41%)
  Pallas kernels  65.9 us (38%)
  starting transfers between devices  27.4 us (16%)
  local copies, waits for them, and re-layouts  4.44 us (3%)
  other arithmetic  2.93 us (2%)
    pallas_call x1, Pallas kernels, scored_sums(): pl.pallas_call(body, out_shape=(jax.ShapeDtypeStruct((blocks, 1, BLOCK),...  65.9 us
    ppermute x6, waiting for transfers between devices, moved(): return lax.ppermute(value, 'blk', [(i, i ^ 2) for i in range(count)])  37.3 us
    ppermute x6, waiting for transfers between devices, moved(): lax.ppermute(value, 'blk', [(i, (i + shift) % count) for i in range(count)])  29.4 us
    ppermute x6, starting transfers between devices, moved(): lax.ppermute(value, 'blk', [(i, (i + shift) % count) for i in range(count)])  17.8 us
    ppermute x6, starting transfers between devices, moved(): return lax.ppermute(value, 'blk', [(i, i ^ 2) for i in range(count)])  7.43 us
    ppermute x14, waiting for transfers between devices, other_core(): return lax.ppermute(value, 'blk', [(i, i ^ 1) for i in range(count)])  3.79 us
  transfers between devices with their start and end apart: 26, of which 15 were waited for; matrix products, arithmetic and copies ran while one was open for 1% of the time, Pallas kernels for 0%

profile of v2, /device:TPU:0, one launch (start us, length us, event | category | flops | bytes accessed | tf_op | source)
XLA Modules:
  0.0 171.9 jit_solution(6360002333580865232)
XLA Ops:
  0.6 3.1 %collective-permute-start = (bf16[256,768]{1,0:T(8,128)(2,1)}, bf16[256,768]{1,0:T(8,128)(2,1)S(1)}, u32[]{:S(2)}, u32[]{:S(2)}) collective-permute-start(bf16[256,768]{1,0:T(8,128)(2,1)} %refs_2_.1), channel_id=1, source_target_pairs={{0,4},{1,5},{2,6},{3,7},{4,8},{5,9},{6,10},{7,11},{8,12},{9,13},{1... | collective-permute-start | bytes 1179656 | tf_op jit(solution)/shard_map/ppermute | solution.py:48
  3.7 2.1 %collective-permute-start.2 = (bf16[256,768]{1,0:T(8,128)(2,1)}, bf16[256,768]{1,0:T(8,128)(2,1)S(1)}, u32[]{:S(2)}, u32[]{:S(2)}) collective-permute-start(bf16[256,768]{1,0:T(8,128)(2,1)} %refs_2_.1), channel_id=1, source_target_pairs={{0,12},{1,13},{2,14},{3,15},{4,0},{5,1},{6,2},{7,3},{8,4},{9,5},{1... | collective-permute-start | bytes 1179656 | tf_op jit(solution)/shard_map/ppermute | solution.py:48
  5.8 10.1 %collective-permute-done.refs_3_ = bf16[256,768]{1,0:T(8,128)(2,1)S(1)} collective-permute-done((bf16[256,768]{1,0:T(8,128)(2,1)}, bf16[256,768]{1,0:T(8,128)(2,1)S(1)}, u32[]{:S(2)}, u32[]{:S(2)}) %collective-permute-start) | collective-permute-done | bytes 393248 | tf_op jit(solution)/shard_map/ppermute | solution.py:48
  15.9 1.8 %collective-permute-start.3 = (bf16[256,768]{1,0:T(8,128)(2,1)S(1)}, bf16[256,768]{1,0:T(8,128)(2,1)S(1)}, u32[]{:S(2)}, u32[]{:S(2)}) collective-permute-start(bf16[256,768]{1,0:T(8,128)(2,1)S(1)} %collective-permute-done.refs_3_), channel_id=1, source_target_pairs={{0,2},{1,3},{2,0},{3,1},{4,6},{5,7},{6,4},{7,5},{8,10},{9,11},{10,... | collective-permute-start | bytes 1179656 | tf_op jit(solution)/shard_map/ppermute | solution.py:47
  18.0 5.0 %collective-permute-done.2.refs_5_ = bf16[256,768]{1,0:T(8,128)(2,1)S(1)} collective-permute-done((bf16[256,768]{1,0:T(8,128)(2,1)}, bf16[256,768]{1,0:T(8,128)(2,1)S(1)}, u32[]{:S(2)}, u32[]{:S(2)}) %collective-permute-start.2) | collective-permute-done | bytes 393248 | tf_op jit(solution)/shard_map/ppermute | solution.py:48
  22.9 1.5 collective-permute-start.4
  24.4 3.5 %collective-permute-done.3.refs_6_ = bf16[256,768]{1,0:T(8,128)(2,1)S(1)} collective-permute-done((bf16[256,768]{1,0:T(8,128)(2,1)S(1)}, bf16[256,768]{1,0:T(8,128)(2,1)S(1)}, u32[]{:S(2)}, u32[]{:S(2)}) %collective-permute-start.3) | collective-permute-done | bytes 393248 | tf_op jit(solution)/shard_map/ppermute | solution.py:47
  28.0 8.4 %collective-permute-done.1.refs_4_ = bf16[256,768]{1,0:T(8,128)(2,1)S(1)} collective-permute-done((bf16[256,768]{1,0:T(8,128)(2,1)}, bf16[256,768]{1,0:T(8,128)(2,1)S(1)}, u32[]{:S(2)}, u32[]{:S(2)}) %collective-permute-start.1) | collective-permute-done | bytes 393248 | tf_op jit(solution)/shard_map/ppermute | solution.py:47
  36.4 0.5 collective-permute-start.10
  36.9 5.3 %collective-permute-done.4.refs_7_ = bf16[256,768]{1,0:T(8,128)(2,1)S(1)} collective-permute-done((bf16[256,768]{1,0:T(8,128)(2,1)S(1)}, bf16[256,768]{1,0:T(8,128)(2,1)S(1)}, u32[]{:S(2)}, u32[]{:S(2)}) %collective-permute-start.4) | collective-permute-done | bytes 393248 | tf_op jit(solution)/shard_map/ppermute | solution.py:47
  42.3 0.5 collective-permute-start.12
  42.8 0.7 fusion.27
  43.7 0.4 collective-permute-done.11.refs_14_
  44.1 0.6 collective-permute-done.12.refs_15_
  44.7 1.0 copy-done
  45.7 65.9 %scored_sums.1 = (f32[16,1,256]{2,1,0:T(1,128)}, f32[8,264,768]{2,1,0:T(8,128)}, f32[8,264,768]{2,1,0:T(8,128)}) custom-call(s32[96]{0:T(128)S(1)} %reshape.19.refs_0_, bf16[4096,768]{1,0:T(8,128)(2,1)} %refs_1_.1, bf16[256,768]{1,0:T(8,128)(2,1)S(1)} %copy-done, bf16[256,768]{1,0:T(8,128)(2,1)S(1)} %collective-permute-done.refs_3_, ...), custom_call_target="tpu_custom_call" | custom-call | flops 19327352832 | bytes 22806528 | tf_op jit(solution)/shard_map/scored_sums/pallas_call | solution.py:158
  111.6 3.3 %slice_bitcast_fusion.4 = (f32[264,768]{1,0:T(8,128)S(1)}, f32[264,768]{1,0:T(8,128)S(1)}, f32[264,768]{1,0:T(8,128)S(1)}, f32[264,768]{1,0:T(8,128)S(1)}, f32[2...) fusion(f32[8,264,768]{2,1,0:T(8,128)} %get-tuple-element.6), kind=kLoop, calls=%fused_computation.31 | loop fusion | bytes 11354112 | tf_op jit(solution)/shard_map/squeeze | solution.py:192
  115.1 0.4 collective-permute-start.22
  116.0 1.3 collective-permute-done.15
  117.4 1.9 %collective-permute-start.16 = (f16[264,768]{1,0:T(8,128)(2,1)S(1)}, f16[264,768]{1,0:T(8,128)(2,1)S(1)}, u32[]{:S(2)}, u32[]{:S(2)}) collective-permute-start(f16[264,768]{1,0:T(8,128)(2,1)S(1)} %fusion.11), channel_id=1, source_target_pairs={{0,2},{1,3},{2,0},{3,1},{4,6},{5,7},{6,4},{7,5},{8,10},{9,11},{10,... | collective-permute-start | bytes 1216520 | tf_op jit(solution)/shard_map/ppermute | solution.py:47
  119.6 1.2 collective-permute-done.14
  120.8 8.3 %collective-permute-done.16 = f16[264,768]{1,0:T(8,128)(2,1)S(1)} collective-permute-done((f16[264,768]{1,0:T(8,128)(2,1)S(1)}, f16[264,768]{1,0:T(8,128)(2,1)S(1)}, u32[]{:S(2)}, u32[]{:S(2)}) %collective-permute-start.16) | collective-permute-done | bytes 405536 | tf_op jit(solution)/shard_map/ppermute | solution.py:47
  129.1 0.4 fusion.14
  129.5 7.8 %collective-permute-start.23 = (f16[264,768]{1,0:T(8,128)(2,1)S(1)}, f16[264,768]{1,0:T(8,128)(2,1)S(1)}, u32[]{:S(2)}, u32[]{:S(2)}) collective-permute-start(f16[264,768]{1,0:T(8,128)(2,1)S(1)} %get-tuple-element.9), channel_id=1, source_target_pairs={{0,12},{1,13},{2,14},{3,15},{4,0},{5,1},{6,2},{7,3},{8,4},{9,5},{1... | collective-permute-start | bytes 1216520 | tf_op jit(solution)/shard_map/ppermute | solution.py:48
  137.4 8.4 %collective-permute-done.23 = f16[264,768]{1,0:T(8,128)(2,1)S(1)} collective-permute-done((f16[264,768]{1,0:T(8,128)(2,1)S(1)}, f16[264,768]{1,0:T(8,128)(2,1)S(1)}, u32[]{:S(2)}, u32[]{:S(2)}) %collective-permute-start.23) | collective-permute-done | bytes 405536 | tf_op jit(solution)/shard_map/ppermute | solution.py:48
  146.0 1.6 collective-permute-start.24
  147.6 0.5 collective-permute-start.17
  148.4 9.9 %collective-permute-done.24 = f16[264,768]{1,0:T(8,128)(2,1)S(1)} collective-permute-done((f16[264,768]{1,0:T(8,128)(2,1)S(1)}, f16[264,768]{1,0:T(8,128)(2,1)S(1)}, u32[]{:S(2)}, u32[]{:S(2)}) %collective-permute-start.24) | collective-permute-done | bytes 405536 | tf_op jit(solution)/shard_map/ppermute | solution.py:47
  158.5 4.3 %collective-permute-start.25 = (f16[264,768]{1,0:T(8,128)(2,1)S(1)}, f16[264,768]{1,0:T(8,128)(2,1)S(1)}, u32[]{:S(2)}, u32[]{:S(2)}) collective-permute-start(f16[264,768]{1,0:T(8,128)(2,1)S(1)} %fusion.7), channel_id=1, source_target_pairs={{0,12},{1,13},{2,14},{3,15},{4,0},{5,1},{6,2},{7,3},{8,4},{9,5},{1... | collective-permute-start | bytes 1216520 | tf_op jit(solution)/shard_map/ppermute | solution.py:48
  162.9 1.8 %collective-permute-done.19 = f16[264,768]{1,0:T(8,128)(2,1)S(1)} collective-permute-done((f16[264,768]{1,0:T(8,128)(2,1)S(1)}, f16[264,768]{1,0:T(8,128)(2,1)S(1)}, u32[]{:S(2)}, u32[]{:S(2)}) %collective-permute-start.19) | collective-permute-done | bytes 405536 | tf_op jit(solution)/shard_map/ppermute | solution.py:47
  164.7 5.9 %collective-permute-done.25 = f16[264,768]{1,0:T(8,128)(2,1)S(1)} collective-permute-done((f16[264,768]{1,0:T(8,128)(2,1)S(1)}, f16[264,768]{1,0:T(8,128)(2,1)S(1)}, u32[]{:S(2)}, u32[]{:S(2)}) %collective-permute-start.25) | collective-permute-done | bytes 405536 | tf_op jit(solution)/shard_map/ppermute | solution.py:48
  170.9 1.0 fusion.20
  (36 shorter events, 2.6 us)
Async XLA Ops:
  0.6 15.3 %collective-permute-start = (bf16[256,768]{1,0:T(8,128)(2,1)}, bf16[256,768]{1,0:T(8,128)(2,1)S(1)}, u32[]{:S(2)}, u32[]{:S(2)}) collective-permute-start(bf16[256,768]{1,0:T(8,128)(2,1)} %refs_2_.1), channel_id=1, source_target_pairs={{0,4},{1,5},{2,6},{3,7},{4,8},{5,9},{6,10},{7,11},{8,12},{9,13},{1... | collective-permute-start | bytes 1179656 | tf_op jit(solution)/shard_map/ppermute | solution.py:48
  3.7 19.2 %collective-permute-start.2 = (bf16[256,768]{1,0:T(8,128)(2,1)}, bf16[256,768]{1,0:T(8,128)(2,1)S(1)}, u32[]{:S(2)}, u32[]{:S(2)}) collective-permute-start(bf16[256,768]{1,0:T(8,128)(2,1)} %refs_2_.1), channel_id=1, source_target_pairs={{0,12},{1,13},{2,14},{3,15},{4,0},{5,1},{6,2},{7,3},{8,4},{9,5},{1... | collective-permute-start | bytes 1179656 | tf_op jit(solution)/shard_map/ppermute | solution.py:48
  15.9 12.1 %collective-permute-start.3 = (bf16[256,768]{1,0:T(8,128)(2,1)S(1)}, bf16[256,768]{1,0:T(8,128)(2,1)S(1)}, u32[]{:S(2)}, u32[]{:S(2)}) collective-permute-start(bf16[256,768]{1,0:T(8,128)(2,1)S(1)} %collective-permute-done.refs_3_), channel_id=1, source_target_pairs={{0,2},{1,3},{2,0},{3,1},{4,6},{5,7},{6,4},{7,5},{8,10},{9,11},{10,... | collective-permute-start | bytes 1179656 | tf_op jit(solution)/shard_map/ppermute | solution.py:47
  17.7 10.3 %collective-permute-start.6 = (bf16[256,768]{1,0:T(8,128)(2,1)}, bf16[256,768]{1,0:T(8,128)(2,1)S(1)}, u32[]{:S(2)}, u32[]{:S(2)}) collective-permute-start(bf16[256,768]{1,0:T(8,128)(2,1)} %refs_2_.1), channel_id=1, source_target_pairs={{0,1},{1,0},{2,3},{3,2},{4,5},{5,4},{6,7},{7,6},{8,9},{9,8},{10,11... | collective-permute-start | bytes 1179656 | tf_op jit(solution)/shard_map/ppermute | solution.py:53
  17.7 18.7 %collective-permute-start.1 = (bf16[256,768]{1,0:T(8,128)(2,1)}, bf16[256,768]{1,0:T(8,128)(2,1)S(1)}, u32[]{:S(2)}, u32[]{:S(2)}) collective-permute-start(bf16[256,768]{1,0:T(8,128)(2,1)} %refs_2_.1), channel_id=1, source_target_pairs={{0,2},{1,3},{2,0},{3,1},{4,6},{5,7},{6,4},{7,5},{8,10},{9,11},{10,... | collective-permute-start | bytes 1179656 | tf_op jit(solution)/shard_map/ppermute | solution.py:47
  22.9 13.5 %collective-permute-start.9 = (bf16[256,768]{1,0:T(8,128)(2,1)S(1)}, bf16[256,768]{1,0:T(8,128)(2,1)S(1)}, u32[]{:S(2)}, u32[]{:S(2)}) collective-permute-start(bf16[256,768]{1,0:T(8,128)(2,1)S(1)} %collective-permute-done.2.refs_5_), channel_id=1, source_target_pairs={{0,1},{1,0},{2,3},{3,2},{4,5},{5,4},{6,7},{7,6},{8,9},{9,8},{10,11... | collective-permute-start | bytes 1179656 | tf_op jit(solution)/shard_map/ppermute | solution.py:53
  22.9 19.3 %collective-permute-start.4 = (bf16[256,768]{1,0:T(8,128)(2,1)S(1)}, bf16[256,768]{1,0:T(8,128)(2,1)S(1)}, u32[]{:S(2)}, u32[]{:S(2)}) collective-permute-start(bf16[256,768]{1,0:T(8,128)(2,1)S(1)} %collective-permute-done.2.refs_5_), channel_id=1, source_target_pairs={{0,2},{1,3},{2,0},{3,1},{4,6},{5,7},{6,4},{7,5},{8,10},{9,11},{10,... | collective-permute-start | bytes 1179656 | tf_op jit(solution)/shard_map/ppermute | solution.py:47
  28.0 14.3 %collective-permute-start.5 = (bf16[256,768]{1,0:T(8,128)(2,1)S(1)}, bf16[256,768]{1,0:T(8,128)(2,1)S(1)}, u32[]{:S(2)}, u32[]{:S(2)}) collective-permute-start(bf16[256,768]{1,0:T(8,128)(2,1)S(1)} %collective-permute-done.3.refs_6_), channel_id=1, source_target_pairs={{0,4},{1,5},{2,6},{3,7},{4,8},{5,9},{6,10},{7,11},{8,12},{9,13},{1... | collective-permute-start | bytes 1179656 | tf_op jit(solution)/shard_map/ppermute | solution.py:48
  28.0 15.7 %collective-permute-start.7 = (bf16[256,768]{1,0:T(8,128)(2,1)S(1)}, bf16[256,768]{1,0:T(8,128)(2,1)S(1)}, u32[]{:S(2)}, u32[]{:S(2)}) collective-permute-start(bf16[256,768]{1,0:T(8,128)(2,1)S(1)} %collective-permute-done.refs_3_), channel_id=1, source_target_pairs={{0,1},{1,0},{2,3},{3,2},{4,5},{5,4},{6,7},{7,6},{8,9},{9,8},{10,11... | collective-permute-start | bytes 1179656 | tf_op jit(solution)/shard_map/ppermute | solution.py:53
  36.4 7.2 %collective-permute-start.8 = (bf16[256,768]{1,0:T(8,128)(2,1)S(1)}, bf16[256,768]{1,0:T(8,128)(2,1)}, u32[]{:S(2)}, u32[]{:S(2)}) collective-permute-start(bf16[256,768]{1,0:T(8,128)(2,1)S(1)} %collective-permute-done.1.refs_4_), channel_id=1, source_target_pairs={{0,1},{1,0},{2,3},{3,2},{4,5},{5,4},{6,7},{7,6},{8,9},{9,8},{10,11... | collective-permute-start | bytes 1179656 | tf_op jit(solution)/shard_map/ppermute | solution.py:53
  36.4 7.7 %collective-permute-start.10 = (bf16[256,768]{1,0:T(8,128)(2,1)S(1)}, bf16[256,768]{1,0:T(8,128)(2,1)}, u32[]{:S(2)}, u32[]{:S(2)}) collective-permute-start(bf16[256,768]{1,0:T(8,128)(2,1)S(1)} %collective-permute-done.3.refs_6_), channel_id=1, source_target_pairs={{0,1},{1,0},{2,3},{3,2},{4,5},{5,4},{6,7},{7,6},{8,9},{9,8},{10,11... | collective-permute-start | bytes 1179656 | tf_op jit(solution)/shard_map/ppermute | solution.py:53
  42.3 1.9 %collective-permute-start.11 = (bf16[256,768]{1,0:T(8,128)(2,1)S(1)}, bf16[256,768]{1,0:T(8,128)(2,1)}, u32[]{:S(2)}, u32[]{:S(2)}) collective-permute-start(bf16[256,768]{1,0:T(8,128)(2,1)S(1)} %collective-permute-done.4.refs_7_), channel_id=1, source_target_pairs={{0,1},{1,0},{2,3},{3,2},{4,5},{5,4},{6,7},{7,6},{8,9},{9,8},{10,11... | collective-permute-start | bytes 1179656 | tf_op jit(solution)/shard_map/ppermute | solution.py:53
  42.3 2.4 %collective-permute-start.12 = (bf16[256,768]{1,0:T(8,128)(2,1)S(1)}, bf16[256,768]{1,0:T(8,128)(2,1)}, u32[]{:S(2)}, u32[]{:S(2)}) collective-permute-start(bf16[256,768]{1,0:T(8,128)(2,1)S(1)} %collective-permute-done.5.refs_8_), channel_id=1, source_target_pairs={{0,1},{1,0},{2,3},{3,2},{4,5},{5,4},{6,7},{7,6},{8,9},{9,8},{10,11... | collective-permute-start | bytes 1179656 | tf_op jit(solution)/shard_map/ppermute | solution.py:53
  44.7 1.0 copy-start
  111.6 5.7 %copy-start.1 = (f32[8,264,768]{2,1,0:T(8,128)S(1)}, f32[8,264,768]{2,1,0:T(8,128)}, u32[]{:S(2)}) copy-start(f32[8,264,768]{2,1,0:T(8,128)} %get-tuple-element.5) | copy-start | bytes 19464196
  114.9 2.4 %collective-permute-start.15 = (f32[264,768]{1,0:T(8,128)S(1)}, f32[264,768]{1,0:T(8,128)S(1)}, u32[]{:S(2)}, u32[]{:S(2)}) collective-permute-start(f32[264,768]{1,0:T(8,128)S(1)} %get-tuple-element.11), channel_id=1, source_target_pairs={{0,1},{1,0},{2,3},{3,2},{4,5},{5,4},{6,7},{7,6},{8,9},{9,8},{10,11... | collective-permute-start | bytes 2433032 | tf_op jit(solution)/shard_map/ppermute | solution.py:53
  115.1 4.2 %collective-permute-start.22 = (f32[264,768]{1,0:T(8,128)S(1)}, f32[264,768]{1,0:T(8,128)S(1)}, u32[]{:S(2)}, u32[]{:S(2)}) collective-permute-start(f32[264,768]{1,0:T(8,128)S(1)} %get-tuple-element.12), channel_id=1, source_target_pairs={{0,1},{1,0},{2,3},{3,2},{4,5},{5,4},{6,7},{7,6},{8,9},{9,8},{10,11... | collective-permute-start | bytes 2433032 | tf_op jit(solution)/shard_map/ppermute | solution.py:53
  115.5 4.1 %collective-permute-start.18 = (f32[264,768]{1,0:T(8,128)S(1)}, f32[264,768]{1,0:T(8,128)S(1)}, u32[]{:S(2)}, u32[]{:S(2)}) collective-permute-start(f32[264,768]{1,0:T(8,128)S(1)} %get-tuple-element.15), channel_id=1, source_target_pairs={{0,1},{1,0},{2,3},{3,2},{4,5},{5,4},{6,7},{7,6},{8,9},{9,8},{10,11... | collective-permute-start | bytes 2433032 | tf_op jit(solution)/shard_map/ppermute | solution.py:53
  115.6 5.2 %collective-permute-start.14 = (f32[264,768]{1,0:T(8,128)S(1)}, f32[264,768]{1,0:T(8,128)S(1)}, u32[]{:S(2)}, u32[]{:S(2)}) collective-permute-start(f32[264,768]{1,0:T(8,128)S(1)} %get-tuple-element.16), channel_id=1, source_target_pairs={{0,1},{1,0},{2,3},{3,2},{4,5},{5,4},{6,7},{7,6},{8,9},{9,8},{10,11... | collective-permute-start | bytes 2433032 | tf_op jit(solution)/shard_map/ppermute | solution.py:53
  117.4 11.7 %collective-permute-start.16 = (f16[264,768]{1,0:T(8,128)(2,1)S(1)}, f16[264,768]{1,0:T(8,128)(2,1)S(1)}, u32[]{:S(2)}, u32[]{:S(2)}) collective-permute-start(f16[264,768]{1,0:T(8,128)(2,1)S(1)} %fusion.11), channel_id=1, source_target_pairs={{0,2},{1,3},{2,0},{3,1},{4,6},{5,7},{6,4},{7,5},{8,10},{9,11},{10,... | collective-permute-start | bytes 1216520 | tf_op jit(solution)/shard_map/ppermute | solution.py:47
  119.3 18.1 %collective-permute-start.21 = (f32[264,768]{1,0:T(8,128)S(1)}, f32[264,768]{1,0:T(8,128)S(1)}, u32[]{:S(2)}, u32[]{:S(2)}) collective-permute-start(f32[264,768]{1,0:T(8,128)S(1)} %get-tuple-element.13), channel_id=1, source_target_pairs={{0,1},{1,0},{2,3},{3,2},{4,5},{5,4},{6,7},{7,6},{8,9},{9,8},{10,11... | collective-permute-start | bytes 2433032 | tf_op jit(solution)/shard_map/ppermute | solution.py:53
  129.5 16.2 %collective-permute-start.23 = (f16[264,768]{1,0:T(8,128)(2,1)S(1)}, f16[264,768]{1,0:T(8,128)(2,1)S(1)}, u32[]{:S(2)}, u32[]{:S(2)}) collective-permute-start(f16[264,768]{1,0:T(8,128)(2,1)S(1)} %get-tuple-element.9), channel_id=1, source_target_pairs={{0,12},{1,13},{2,14},{3,15},{4,0},{5,1},{6,2},{7,3},{8,4},{9,5},{1... | collective-permute-start | bytes 1216520 | tf_op jit(solution)/shard_map/ppermute | solution.py:48
  137.4 11.1 %collective-permute-start.20 = (f32[264,768]{1,0:T(8,128)S(1)}, f32[264,768]{1,0:T(8,128)S(1)}, u32[]{:S(2)}, u32[]{:S(2)}) collective-permute-start(f32[264,768]{1,0:T(8,128)S(1)} %get-tuple-element.14), channel_id=1, source_target_pairs={{0,1},{1,0},{2,3},{3,2},{4,5},{5,4},{6,7},{7,6},{8,9},{9,8},{10,11... | collective-permute-start | bytes 2433032 | tf_op jit(solution)/shard_map/ppermute | solution.py:53
  146.0 12.4 %collective-permute-start.24 = (f16[264,768]{1,0:T(8,128)(2,1)S(1)}, f16[264,768]{1,0:T(8,128)(2,1)S(1)}, u32[]{:S(2)}, u32[]{:S(2)}) collective-permute-start(f16[264,768]{1,0:T(8,128)(2,1)S(1)} %fusion.4), channel_id=1, source_target_pairs={{0,2},{1,3},{2,0},{3,1},{4,6},{5,7},{6,4},{7,5},{8,10},{9,11},{10,... | collective-permute-start | bytes 1216520 | tf_op jit(solution)/shard_map/ppermute | solution.py:47
  147.6 15.3 %collective-permute-start.13 = (f32[264,768]{1,0:T(8,128)S(1)}, f32[264,768]{1,0:T(8,128)S(1)}, u32[]{:S(2)}, u32[]{:S(2)}) collective-permute-start(f32[264,768]{1,0:T(8,128)S(1)} %get-tuple-element.17), channel_id=1, source_target_pairs={{0,1},{1,0},{2,3},{3,2},{4,5},{5,4},{6,7},{7,6},{8,9},{9,8},{10,11... | collective-permute-start | bytes 2433032 | tf_op jit(solution)/shard_map/ppermute | solution.py:53
  147.6 15.3 %collective-permute-start.17 = (f16[264,768]{1,0:T(8,128)(2,1)S(1)}, f16[264,768]{1,0:T(8,128)(2,1)S(1)}, u32[]{:S(2)}, u32[]{:S(2)}) collective-permute-start(f16[264,768]{1,0:T(8,128)(2,1)S(1)} %get-tuple-element.8), channel_id=1, source_target_pairs={{0,4},{1,5},{2,6},{3,7},{4,8},{5,9},{6,10},{7,11},{8,12},{9,13},{1... | collective-permute-start | bytes 1216520 | tf_op jit(solution)/shard_map/ppermute | solution.py:48
  148.1 16.6 %collective-permute-start.19 = (f16[264,768]{1,0:T(8,128)(2,1)S(1)}, f16[264,768]{1,0:T(8,128)(2,1)S(1)}, u32[]{:S(2)}, u32[]{:S(2)}) collective-permute-start(f16[264,768]{1,0:T(8,128)(2,1)S(1)} %get-tuple-element.10), channel_id=1, source_target_pairs={{0,2},{1,3},{2,0},{3,1},{4,6},{5,7},{6,4},{7,5},{8,10},{9,11},{10,... | collective-permute-start | bytes 1216520 | tf_op jit(solution)/shard_map/ppermute | solution.py:47
  158.5 12.1 %collective-permute-start.25 = (f16[264,768]{1,0:T(8,128)(2,1)S(1)}, f16[264,768]{1,0:T(8,128)(2,1)S(1)}, u32[]{:S(2)}, u32[]{:S(2)}) collective-permute-start(f16[264,768]{1,0:T(8,128)(2,1)S(1)} %fusion.7), channel_id=1, source_target_pairs={{0,12},{1,13},{2,14},{3,15},{4,0},{5,1},{6,2},{7,3},{8,4},{9,5},{1... | collective-permute-start | bytes 1216520 | tf_op jit(solution)/shard_map/ppermute | solution.py:48
